TPU v7x, 128 devices: a whole 4x4x4 slice. The times are simulated.
128 devices in a mesh: pass: 8 (over y_hi, x), red: 8 (over z, core), grp: 2 (over y_lo).
Axes of the slice: x: 4, y: 4 (y_hi: 2, y_lo: 2; y = y_hi * 2 + y_lo), z: 4, core: 2. Of those that a mesh axis runs over, the one named last changes fastest.
Arguments:
- query_lex: bfloat16 [1536, 16384], P(None, 'red')
- query_dense: bfloat16 [1536, 4096], P(None, 'red')
- passage_lex: bfloat16 [8192, 16384], P(('pass', 'grp'), 'red'), may hold values from 0 to 0.47
- passage_dense: bfloat16 [8192, 4096], P(('pass', 'grp'), 'red'), may hold values from -1.33 to 1.33
- positives: int32 [1536], replicated, may hold values from 0 to 8191
Outputs:
- loss_rows: float32 [1536], P('red')
- grad_query_lex: float32 [1536, 16384], P(('pass', 'grp'), 'red')
- grad_query_dense: float32 [1536, 4096], P(('pass', 'grp'), 'red')
- grad_passage_lex: float32 [8192, 16384], P(('pass', 'grp'), 'red')
- grad_passage_dense: float32 [8192, 4096], P(('pass', 'grp'), 'red')
All inputs are finite; a program needn't handle non-finite values.
Results may differ from a plain program's by a relative error of at most 0.0022.
Values may be sent and summed in bfloat16 or wider, within the bound.
No kernel may reach another device: no remote copies, remote signals or barrier semaphores. Data moves between devices by JAX's collectives and lax.ppermute only.
A program may use at most 128 MiB of HBM per device.

v0:
```python
import jax
import jax.numpy as jnp
from jax import lax
from jax.experimental import pallas as pl
from jax.experimental.pallas import tpu as pltpu
from jax.sharding import Mesh, PartitionSpec as P

RED = ("z", "core")
PLANE = ("yh", "x", "yl")
COLUMN = ("yh", "yl")
NT = (((1,), (1,)), ((), ()))
NN = (((1,), (0,)), ((), ()))


def matmul(first, second, dims):
    return lax.dot_general(first, second, dims, preferred_element_type=jnp.float32)


def half_scores(half, query_lex, query_dense, passage_lex, passage_dense):
    queries, terms = query_lex.shape
    passages, width = passage_dense.shape
    rows = queries // 8
    part = rows // 4

    def body(half_ref, ql, qd, pl_, pd, out):
        dense = matmul(qd[...], pd[...], NT)
        lexical = matmul(ql[...], pl_[...], NT)
        for x in range(2):
            own = slice(x * rows, (x + 1) * rows)
            out[:, x, :, :passages] = dense[own].reshape(4, part, passages)
            out[:, x, :, passages:] = lexical[own].reshape(4, part, passages)

    return pl.pallas_call(
        body,
        out_shape=jax.ShapeDtypeStruct((4, 4, part, 2 * passages), jnp.float32),
        grid_spec=pltpu.PrefetchScalarGridSpec(
            num_scalar_prefetch=1,
            grid=(2,),
            in_specs=[
                pl.BlockSpec((2 * rows, terms), lambda i, h: (h[0] * 2 + i, 0)),
                pl.BlockSpec((2 * rows, width), lambda i, h: (h[0] * 2 + i, 0)),
                pl.BlockSpec((passages, terms), lambda i, h: (0, 0)),
                pl.BlockSpec((passages, width), lambda i, h: (0, 0)),
            ],
            out_specs=pl.BlockSpec((4, 2, part, 2 * passages), lambda i, h: (0, i, 0, 0)),
        ),
        name="half_scores",
    )(half, query_lex, query_dense, passage_lex, passage_dense)


def query_gradients(place, grads, partner, passage_lex, passage_dense):
    part, passages = grads.shape[2], grads.shape[3] // 2
    terms, width = passage_lex.shape[2], passage_dense[0].shape[1]
    tiles = terms // width
    rows, own_rows = 8 * part, 2 * part

    def body(place_ref, g, other, lex, d0, d1, d2, d3, out, own, left, sums):
        dense = (d0, d1, d2, d3)
        step = pl.program_id(0)

        def arrange(low, lines):
            for source, c in ((g, place_ref[1]), (other, 1 - place_ref[1])):
                at = pl.multiple_of(c * 4 * part, 4 * part)
                for x in range(4):
                    left[pl.ds(at, 4 * part), x * passages : (x + 1) * passages] = source[
                        :, lines[x], :, low : low + passages
                    ].reshape(4 * part, passages)

        @pl.when(step == 0)
        def _():
            arrange(passages, [place_ref[2 + x] for x in range(4)])

        def finish():
            out[...] = sums[...].astype(out.dtype)
            at = pl.multiple_of(place_ref[0] * own_rows, own_rows)
            own[...] = sums[pl.ds(at, own_rows), :]

        @pl.when(step < tiles)
        def _():
            sums[...] = matmul(left[...], lex[...].reshape(4 * passages, width), NN)
            finish()

        @pl.when(step == tiles)
        def _():
            arrange(0, range(4))
            acc = None
            for x in range(4):
                at = slice(x * passages, (x + 1) * passages)
                term = matmul(left[:, at], dense[x][...], NN)
                acc = term if acc is None else acc + term
            sums[...] = acc
            finish()

    return pl.pallas_call(
        body,
        out_shape=(
            jax.ShapeDtypeStruct((rows, terms + width), jnp.bfloat16),
            jax.ShapeDtypeStruct((own_rows, terms + width), jnp.float32),
        ),
        grid_spec=pltpu.PrefetchScalarGridSpec(
            num_scalar_prefetch=1,
            grid=(tiles + 1,),
            in_specs=[
                pl.BlockSpec(grads.shape, lambda i, h: (0, 0, 0, 0)),
                pl.BlockSpec(grads.shape, lambda i, h: (0, 0, 0, 0)),
                pl.BlockSpec(
                    (4, passages, width), lambda i, h: (0, 0, jnp.minimum(i, tiles - 1))
                ),
            ]
            + [pl.BlockSpec((passages, width), lambda i, h: (0, 0))] * 4,
            out_specs=(
                pl.BlockSpec((rows, width), lambda i, h: (0, i)),
                pl.BlockSpec((own_rows, width), lambda i, h: (0, i)),
            ),
            scratch_shapes=[
                pltpu.VMEM((rows, 4 * passages), jnp.bfloat16),
                pltpu.VMEM((rows, width), jnp.float32),
            ],
        ),
        name="query_gradients",
    )(place, grads, partner, passage_lex, *passage_dense)


def passage_gradients(grads, query_lex, query_dense):
    part, passages = grads.shape[3], grads.shape[4] // 2
    queries, terms = query_lex.shape
    width = query_dense.shape[1]
    tiles = terms // width

    def body(g, ql, qd, out_lex, out_dense, left):
        step = pl.program_id(0)

        def arrange(low):
            blocks = [
                g[:, block // 4, block % 4, :, low : low + passages].reshape(4 * part, passages)
                for block in range(8)
            ]
            left[...] = jnp.concatenate(blocks, axis=0).T

        @pl.when(step == 0)
        def _():
            arrange(passages)

        @pl.when(step == tiles)
        def _():
            arrange(0)

        @pl.when(step < tiles)
        def _():
            out_lex[...] = matmul(left[...], ql[...], NN)

        @pl.when(step == tiles)
        def _():
            out_dense[...] = matmul(left[...], qd[...], NN)

    return pl.pallas_call(
        body,
        grid=(tiles + 1,),
        out_shape=(
            jax.ShapeDtypeStruct((passages, terms), jnp.float32),
            jax.ShapeDtypeStruct((passages, width), jnp.float32),
        ),
        in_specs=[
            pl.BlockSpec(grads.shape, lambda i: (0, 0, 0, 0, 0)),
            pl.BlockSpec((queries, width), lambda i: (0, jnp.minimum(i, tiles - 1))),
            pl.BlockSpec((queries, width), lambda i: (0, 0)),
        ],
        out_specs=(
            pl.BlockSpec((passages, width), lambda i: (0, jnp.minimum(i, tiles - 1))),
            pl.BlockSpec((passages, width), lambda i: (0, 0)),
        ),
        scratch_shapes=[pltpu.VMEM((passages, queries), jnp.bfloat16)],
        name="passage_gradients",
    )(grads, query_lex, query_dense)


def to_line(value, axis):
    return lax.all_to_all(
        jnp.broadcast_to(value[None], (4, *value.shape)), axis, 0, 0, tiled=True
    )


def step(query_lex, query_dense, passage_lex, passage_dense, positives):
    core = lax.axis_index("core")
    zed = lax.axis_index("z")
    ex = lax.axis_index("x")
    queries = query_lex.shape[0]
    local_passages = passage_lex.shape[0]
    rows = queries // 8
    part = rows // 4

    line_lex = lax.all_gather(passage_lex, "x", axis=0)

    def scores_of(half):
        return half_scores(
            half.astype(jnp.int32)[None], query_lex, query_dense, passage_lex, passage_dense
        )

    arrived = lax.ppermute(scores_of(1 - core), "core", [(0, 1), (1, 0)])
    both = arrived + scores_of(core)

    def shifted(value, k):
        return lax.ppermute(value, "x", [(x, (x + k) % 4) for x in range(4)])

    both, passage_later = lax.optimization_barrier((both, passage_dense))
    pieces = lax.all_to_all(both, "z", 0, 0, tiled=True)
    near_dense = [shifted(passage_later, 1), shifted(passage_later, 3)]
    far_dense = shifted(passage_later, 2)
    line_dense = [passage_dense, *near_dense, far_dense]
    scores4 = pieces.sum(axis=0)
    scores2 = scores4.reshape(rows, 2 * local_passages)
    dense = scores2[:, :local_passages]
    lexical = scores2[:, local_passages:]
    line_scores = [lax.dynamic_index_in_dim(scores4, ex, 0, keepdims=False)]
    for k in (1, 3, 2):
        part_scores = lax.dynamic_index_in_dim(scores4, (ex + k) % 4, 0, keepdims=False)
        line_scores.append(shifted(part_scores, k))

    mine = lax.dynamic_slice(
        positives.reshape(2, 4, 4, part), (core, 0, zed, 0), (1, 4, 1, part)
    ).reshape(rows)
    first_column = lax.axis_index(PLANE) * local_passages
    columns = first_column + lax.broadcasted_iota(jnp.int32, (1, local_passages), 1)
    target = (mine[:, None] == columns).astype(jnp.float32)
    joined = dense + 0.3 * lexical
    scores = (joined, dense, lexical)
    highest = [jnp.max(s, axis=1) for s in scores]
    powers = [jnp.exp(s - h[:, None]) for s, h in zip(scores, highest)]
    stats = (
        highest
        + [jnp.sum(p, axis=1) for p in powers]
        + [
            jnp.sum(powers[0] * (joined - dense), axis=1),
            jnp.sum(powers[0] * (joined - lexical), axis=1),
        ]
        + [jnp.sum(target * s, axis=1) for s in scores]
    )
    stats = jnp.stack(stats)
    stats = lax.all_to_all(
        jnp.broadcast_to(stats[None], (16, *stats.shape)), PLANE, 0, 0, tiled=True
    )
    top = stats[:, 0:3].max(axis=0)
    factor = jnp.exp(stats[:, 0:3] - top[None])
    totals = (stats[:, 3:6] * factor).sum(axis=0)
    weighted = (stats[:, 6:8] * factor[:, 0:1]).sum(axis=0)
    picked = stats[:, 8:11].sum(axis=0)
    logs = top + jnp.log(totals)
    kl_dense = weighted[0] / totals[0] - logs[0] + logs[1]
    kl_lex = weighted[1] / totals[0] - logs[0] + logs[2]
    loss = (
        logs[0]
        - picked[0]
        + 0.5 * (logs[1] - picked[1])
        + 0.5 * (logs[2] - picked[2])
        + 0.5 * kl_dense
        + 0.5 * kl_lex
    )

    def gradients(dense, lexical, logs, target):
        joined = dense + 0.3 * lexical
        prob = [jnp.exp(s - log[..., None]) for s, log in zip((joined, dense, lexical), logs)]
        return jnp.concatenate(
            [
                (0.5 * prob[0] + prob[1] - 1.5 * target).astype(jnp.bfloat16),
                (-0.2 * prob[0] + prob[2] - 0.8 * target).astype(jnp.bfloat16),
            ],
            axis=-1,
        )

    grads = gradients(dense, lexical, logs, target).reshape(4, part, 2 * local_passages)
    line_logs = lax.dynamic_index_in_dim(logs.reshape(3, 4, part), ex, 1, keepdims=False)
    line_mine = lax.dynamic_index_in_dim(mine.reshape(4, part), ex, 0, keepdims=False)
    line_grads = []
    for k, both_scores in zip((0, 1, 3, 2), line_scores):
        start = (lax.axis_index("yh") * 4 + (ex + 4 - k) % 4) * 2 + lax.axis_index("yl")
        line_columns = start * local_passages + lax.broadcasted_iota(
            jnp.int32, (1, local_passages), 1
        )
        line_target = (line_mine[:, None] == line_columns).astype(jnp.float32)
        line_grads.append(
            gradients(
                both_scores[:, :local_passages],
                both_scores[:, local_passages:],
                line_logs,
                line_target,
            )
        )
    line_grads = jnp.stack(line_grads)
    line_grads = to_line(line_grads, "z")
    line_grads, grads = lax.optimization_barrier((line_grads, grads))
    partner_grads = lax.ppermute(line_grads, "core", [(0, 1), (1, 0)])
    own_grads = lax.all_gather(grads, RED, axis=0)
    all_loss = lax.all_gather(loss, RED, axis=0)
    shape = (4, 2, 4, part, 2 * local_passages)
    place = lax.axis_index(COLUMN)

    def slot_of(x):
        away = (x + 4 - ex) % 4
        return jnp.where(away == 2, 3, jnp.where(away == 3, 1, away * 2))

    sums, own = query_gradients(
        jnp.stack([place, core] + [slot_of(x) for x in range(4)]).astype(jnp.int32),
        line_grads,
        partner_grads,
        line_lex,
        line_dense,
    )
    sums = lax.all_to_all(sums.reshape(4, 2 * part, -1), COLUMN, 0, 0, tiled=True)
    passage_lex_out, passage_dense_out = passage_gradients(
        own_grads.reshape(shape), query_lex, query_dense
    )
    others = (jnp.arange(4) != place)[:, None, None]

    def summed(low, high):
        wide = jnp.where(others, sums[:, :, low:high].astype(jnp.float32), 0.0)
        return wide.sum(axis=0) + own[:, low:high]

    terms = passage_lex.shape[1]
    query_lex_out = summed(0, terms)
    query_dense_out = summed(terms, sums.shape[2])
    ordered = all_loss.reshape(4, 2, 4, part).transpose(1, 2, 0, 3).reshape(queries)
    loss_rows = lax.dynamic_slice_in_dim(ordered, lax.axis_index(RED) * rows, rows)
    return loss_rows, query_lex_out, query_dense_out, passage_lex_out, passage_dense_out


def solution(mesh):
    fine = Mesh(mesh.devices.reshape(2, 4, 4, 2, 2), ("yh", "x", "z", "core", "yl"))
    return jax.shard_map(
        step,
        mesh=fine,
        in_specs=(P(None, RED), P(None, RED), P(PLANE, RED), P(PLANE, RED), P()),
        out_specs=(P(RED), P(PLANE, RED), P(PLANE, RED), P(PLANE, RED), P(PLANE, RED)),
        check_vma=False,
    )
```

profile of v0, /device:TPU:0, one launch (start us, length us, event | category | flops | bytes accessed | tf_op | source)
XLA Modules:
  0.0 207.3 jit_solution(2572326047190085578)
XLA Ops:
  7.9 5.9 %half_scores.2 = f32[4,4,48,1024]{3,2,1,0:T(8,128)} custom-call(s32[1]{0:T(128)} %bitcast.half_ref, bf16[1536,2048]{1,0:T(8,128)(2,1)} %ql.5, bf16[1536,512]{1,0:T(8,128)(2,1)} %qd.5, bf16[512,2048]{1,0:T(8,128)(2,1)} %pl_.3, bf16[512,512]{1,0:T(8,128)(2,1)} %d0.1), custom_call_target="tpu_custom_call" | custom-call | tf_op jit(solution)/shard_map/half_scores/pallas_call | solution.py:33
  13.8 5.9 %half_scores.3 = f32[4,4,48,1024]{3,2,1,0:T(8,128)} custom-call(s32[1]{0:T(128)} %bitcast.1.half_ref, bf16[1536,2048]{1,0:T(8,128)(2,1)} %ql.5, bf16[1536,512]{1,0:T(8,128)(2,1)} %qd.5, bf16[512,2048]{1,0:T(8,128)(2,1)} %pl_.3, bf16[512,512]{1,0:T(8,128)(2,1)} %d0.1), custom_call_target="tpu_custom_call" | custom-call | tf_op jit(solution)/shard_map/half_scores/pallas_call | solution.py:33
  19.7 4.6 %add.255 = f32[4,4,48,1024]{3,2,1,0:T(8,128)} add(f32[4,4,48,1024]{3,2,1,0:T(8,128)S(1)} %collective-permute-done, f32[4,4,48,1024]{3,2,1,0:T(8,128)} %half_scores.3) | non-fusion elementwise | flops 786432 | bytes 9437184 | tf_op jit(solution)/shard_map/add | solution.py:200
  24.3 5.6 %all-to-all-start = ((f32[4,4,48,1024]{3,2,1,0:T(8,128)}), f32[4,4,48,1024]{3,2,1,0:T(8,128)}, u32[]{:S(2)}, u32[]{:S(2)}) async-start(f32[4,4,48,1024]{3,2,1,0:T(8,128)} %add.255), calls=%async_computation | async-start | bytes 6291456 | tf_op jit(solution)/shard_map/all_to_all | solution.py:206
  30.2 38.4 %all-to-all-done = f32[4,4,48,1024]{3,2,1,0:T(8,128)} async-done(((f32[4,4,48,1024]{3,2,1,0:T(8,128)}), f32[4,4,48,1024]{3,2,1,0:T(8,128)}, u32[]{:S(2)}, u32[]{:S(2)}) %all-to-all-start) | async-done | bytes 3145760 | tf_op jit(solution)/shard_map/all_to_all | solution.py:206
  68.6 2.4 %reduce_sum.126 = f32[4,48,1024]{2,1,0:T(8,128)S(1)} reduce(f32[4,4,48,1024]{3,2,1,0:T(8,128)} %all-to-all-done, f32[]{:T(128)} %constant.148.clone.1), dimensions={0}, to_apply=%region_0.0 | reduce | flops 589824 | bytes 3932164 | tf_op jit(solution)/shard_map/reduce_sum | solution.py:210
  72.1 0.7 broadcast_in_dim.30
  72.8 7.0 %all-to-all-start.1 = ((f32[16,11,192]{2,1,0:T(8,128)}), f32[16,11,192]{2,1,0:T(8,128)S(1)}, u32[]{:S(2)}, u32[]{:S(2)}) async-start(f32[16,11,192]{2,1,0:T(8,128)} %broadcast_in_dim.30), calls=%async_computation.1 | async-start | bytes 524288 | tf_op jit(solution)/shard_map/all_to_all | solution.py:239
  79.9 3.2 %collective-permute-start.2 = (f32[48,1024]{1,0:T(8,128)S(1)}, f32[48,1024]{1,0:T(8,128)S(1)}, u32[]{:S(2)}, u32[]{:S(2)}) collective-permute-start(f32[48,1024]{1,0:T(8,128)S(1)} %get-tuple-element.40), channel_id=1, source_target_pairs={{0,48},{16,0},{32,16},{48,32},{1,49},{17,1},{33,17},{49,33},{2,50}... | collective-permute-start | bytes 589832 | tf_op jit(solution)/shard_map/ppermute | solution.py:203
  83.1 0.9 collective-permute-start.3
  84.0 0.9 collective-permute-start.1
  84.8 6.0 %all-to-all-done.1 = f32[16,11,192]{2,1,0:T(8,128)S(1)} async-done(((f32[16,11,192]{2,1,0:T(8,128)}), f32[16,11,192]{2,1,0:T(8,128)S(1)}, u32[]{:S(2)}, u32[]{:S(2)}) %all-to-all-start.1) | async-done | bytes 135200 | tf_op jit(solution)/shard_map/all_to_all | solution.py:239
  91.7 5.9 %collective-permute-done.2 = f32[48,1024]{1,0:T(8,128)S(1)} collective-permute-done((f32[48,1024]{1,0:T(8,128)S(1)}, f32[48,1024]{1,0:T(8,128)S(1)}, u32[]{:S(2)}, u32[]{:S(2)}) %collective-permute-start.2) | collective-permute-done | bytes 196640 | tf_op jit(solution)/shard_map/ppermute | solution.py:203
  97.7 1.4 collective-permute-done.3
  99.0 3.6 %collective-permute-done.1 = f32[48,1024]{1,0:T(8,128)S(1)} collective-permute-done((f32[48,1024]{1,0:T(8,128)S(1)}, f32[48,1024]{1,0:T(8,128)S(1)}, u32[]{:S(2)}, u32[]{:S(2)}) %collective-permute-start.1) | collective-permute-done | bytes 196640 | tf_op jit(solution)/shard_map/ppermute | solution.py:203
  103.1 1.3 broadcast_in_dim.55
  104.4 3.7 %all-to-all-start.2 = ((bf16[4,4,48,1024]{3,2,1,0:T(8,128)(2,1)}), bf16[4,4,48,1024]{3,2,1,0:T(8,128)(2,1)S(1)}, u32[]{:S(2)}, u32[]{:S(2)}) async-start(bf16[4,4,48,1024]{3,2,1,0:T(8,128)(2,1)} %broadcast_in_dim.55), calls=%async_computation.2 | async-start | bytes 3145728 | tf_op jit(solution)/shard_map/all_to_all | solution.py:178
  108.2 0.9 slice.133
  109.1 1.0 fusion.4
  110.1 0.8 pad_maximum_fusion.1
  110.9 17.5 %all-to-all-done.2.g = bf16[4,4,48,1024]{3,2,1,0:T(8,128)(2,1)S(1)} async-done(((bf16[4,4,48,1024]{3,2,1,0:T(8,128)(2,1)}), bf16[4,4,48,1024]{3,2,1,0:T(8,128)(2,1)S(1)}, u32[]{:S(2)}, u32[]{:S(2)}) %all-to-all-start.2) | async-done | bytes 1572896 | tf_op jit(solution)/shard_map/all_to_all | solution.py:178
  128.5 4.2 %collective-permute-start.5 = (bf16[512,512]{1,0:T(8,128)(2,1)S(1)}, bf16[512,512]{1,0:T(8,128)(2,1)S(1)}, u32[]{:S(2)}, u32[]{:S(2)}) collective-permute-start(bf16[512,512]{1,0:T(8,128)(2,1)S(1)} %copy-done.1), channel_id=1, source_target_pairs={{0,16},{16,32},{32,48},{48,0},{1,17},{17,33},{33,49},{49,1},{2,18}... | collective-permute-start | bytes 1572872 | tf_op jit(solution)/shard_map/ppermute | solution.py:203
  133.4 1.5 collective-permute-start.7
  135.5 10.3 %collective-permute-done.5.d1 = bf16[512,512]{1,0:T(8,128)(2,1)S(1)} collective-permute-done((bf16[512,512]{1,0:T(8,128)(2,1)S(1)}, bf16[512,512]{1,0:T(8,128)(2,1)S(1)}, u32[]{:S(2)}, u32[]{:S(2)}) %collective-permute-start.5) | collective-permute-done | bytes 524320 | tf_op jit(solution)/shard_map/ppermute | solution.py:203
  145.8 1.7 collective-permute-done.6.d2
  147.5 10.8 %collective-permute-done.7.d3 = bf16[512,512]{1,0:T(8,128)(2,1)} collective-permute-done((bf16[512,512]{1,0:T(8,128)(2,1)S(1)}, bf16[512,512]{1,0:T(8,128)(2,1)}, u32[]{:S(2)}, u32[]{:S(2)}) %collective-permute-start.7) | collective-permute-done | bytes 524320 | tf_op jit(solution)/shard_map/ppermute | solution.py:203
  158.4 10.9 %query_gradients.1 = (bf16[384,2560]{1,0:T(8,128)(2,1)}, f32[96,2560]{1,0:T(8,128)}) custom-call(s32[6]{0:T(128)} %stack.87.place_ref, bf16[4,4,48,1024]{3,2,1,0:T(8,128)(2,1)} %copy-done, bf16[4,4,48,1024]{3,2,1,0:T(8,128)(2,1)} %collective-permute-done.4.other, bf16[4,512,2048]{2,1,0:T(8,128)(2,1)} %bitcast.60, bf16[512,512]{1,0:T(8,128)(2,1)} %d0.1, ...), custom_call_target="tpu_custom_call" | custom-call | tf_op jit(solution)/shard_map/query_gradients/pallas_call | solution.py:94
  169.3 4.2 %all-to-all-start.3 = ((bf16[4,96,2560]{2,1,0:T(8,128)(2,1)}), bf16[4,96,2560]{2,1,0:T(8,128)(2,1)S(1)}, u32[]{:S(2)}, u32[]{:S(2)}) async-start(bf16[4,96,2560]{2,1,0:T(8,128)(2,1)} %bitcast.62), calls=%async_computation.3 | async-start | bytes 3932160 | tf_op jit(solution)/shard_map/all_to_all | solution.py:308
  173.5 9.1 %all-gather.2 = f32[8,1,192]{2,1,0:T(1,128)S(1)} all-gather(f32[1,1,192]{2,1,0:T(1,128)S(1)} %get-tuple-element.55), channel_id=1, replica_groups=mesh['yh'=2,'x'=4,'z'=4,'core'=2,'yl'=2] {'z','core'}, dimensions={0}, use_global_device_ids=true | all-gather | bytes 6912 | tf_op jit(solution)/shard_map/all_gather | solution.py:293
  183.5 11.1 %passage_gradients.1 = (f32[512,2048]{1,0:T(8,128)}, f32[512,512]{1,0:T(8,128)}) custom-call(bf16[4,2,4,48,1024]{4,3,2,1,0:T(8,128)(2,1)} %bitcast.61, bf16[1536,2048]{1,0:T(8,128)(2,1)} %ql.5, bf16[1536,512]{1,0:T(8,128)(2,1)} %qd.5), custom_call_target="tpu_custom_call" | custom-call | tf_op jit(solution)/shard_map/passage_gradients/pallas_call | solution.py:156
  194.6 3.6 %all-to-all-done.3 = bf16[4,96,2560]{2,1,0:T(8,128)(2,1)S(1)} async-done(((bf16[4,96,2560]{2,1,0:T(8,128)(2,1)}), bf16[4,96,2560]{2,1,0:T(8,128)(2,1)S(1)}, u32[]{:S(2)}, u32[]{:S(2)}) %all-to-all-start.3) | async-done | bytes 1966112 | tf_op jit(solution)/shard_map/all_to_all | solution.py:308
  198.6 1.0 slice_add_fusion
  (62 shorter events, 7.1 us)
Async XLA Ops:
  7.2 151.2 %all-gather.6.cloned.1.call-start = ((), (), s32[]{:S(2)}) async-start(), calls=%async_computation.4 | async-start | bytes 10485760 | tf_op jit(solution)/shard_map/all_gather | solution.py:192
  13.8 5.9 %collective-permute-start = (f32[4,4,48,1024]{3,2,1,0:T(8,128)}, f32[4,4,48,1024]{3,2,1,0:T(8,128)S(1)}, u32[]{:S(2)}, u32[]{:S(2)}) collective-permute-start(f32[4,4,48,1024]{3,2,1,0:T(8,128)} %half_scores.2), channel_id=1, source_target_pairs={{0,2},{2,0},{1,3},{3,1},{4,6},{6,4},{5,7},{7,5},{8,10},{10,8},{9,1... | collective-permute-start | bytes 9437192 | tf_op jit(solution)/shard_map/ppermute | solution.py:199
  24.3 5.6 %copy-start.6 = (s32[1536]{0:T(1024)S(1)}, s32[1536]{0:T(1024)}, u32[]{:S(2)}) copy-start(s32[1536]{0:T(1024)} %param.9) | copy-start | bytes 18436
  24.3 44.3 %all-to-all-start = ((f32[4,4,48,1024]{3,2,1,0:T(8,128)}), f32[4,4,48,1024]{3,2,1,0:T(8,128)}, u32[]{:S(2)}, u32[]{:S(2)}) async-start(f32[4,4,48,1024]{3,2,1,0:T(8,128)} %add.255), calls=%async_computation | async-start | bytes 6291456 | tf_op jit(solution)/shard_map/all_to_all | solution.py:206
  30.1 41.7 %copy-start.5 = (s32[192]{0:T(256)}, s32[192]{0:T(256)S(1)}, u32[]{:S(2)}) copy-start(s32[192]{0:T(256)S(1)} %eq.99) | copy-start | bytes 2308
  72.8 18.0 %all-to-all-start.1 = ((f32[16,11,192]{2,1,0:T(8,128)}), f32[16,11,192]{2,1,0:T(8,128)S(1)}, u32[]{:S(2)}, u32[]{:S(2)}) async-start(f32[16,11,192]{2,1,0:T(8,128)} %broadcast_in_dim.30), calls=%async_computation.1 | async-start | bytes 524288 | tf_op jit(solution)/shard_map/all_to_all | solution.py:239
  79.9 17.6 %collective-permute-start.2 = (f32[48,1024]{1,0:T(8,128)S(1)}, f32[48,1024]{1,0:T(8,128)S(1)}, u32[]{:S(2)}, u32[]{:S(2)}) collective-permute-start(f32[48,1024]{1,0:T(8,128)S(1)} %get-tuple-element.40), channel_id=1, source_target_pairs={{0,48},{16,0},{32,16},{48,32},{1,49},{17,1},{33,17},{49,33},{2,50}... | collective-permute-start | bytes 589832 | tf_op jit(solution)/shard_map/ppermute | solution.py:203
  83.1 15.9 %collective-permute-start.3 = (f32[48,1024]{1,0:T(8,128)S(1)}, f32[48,1024]{1,0:T(8,128)S(1)}, u32[]{:S(2)}, u32[]{:S(2)}) collective-permute-start(f32[48,1024]{1,0:T(8,128)S(1)} %get-tuple-element.39), channel_id=1, source_target_pairs={{0,32},{16,48},{32,0},{48,16},{1,33},{17,49},{33,1},{49,17},{2,34}... | collective-permute-start | bytes 589832 | tf_op jit(solution)/shard_map/ppermute | solution.py:203
  84.0 18.7 %collective-permute-start.1 = (f32[48,1024]{1,0:T(8,128)S(1)}, f32[48,1024]{1,0:T(8,128)S(1)}, u32[]{:S(2)}, u32[]{:S(2)}) collective-permute-start(f32[48,1024]{1,0:T(8,128)S(1)} %get-tuple-element.41), channel_id=1, source_target_pairs={{0,16},{16,32},{32,48},{48,0},{1,17},{17,33},{33,49},{49,1},{2,18}... | collective-permute-start | bytes 589832 | tf_op jit(solution)/shard_map/ppermute | solution.py:203
  104.4 24.1 %copy-start.1 = (bf16[512,512]{1,0:T(8,128)(2,1)S(1)}, bf16[512,512]{1,0:T(8,128)(2,1)}, u32[]{:S(2)}) copy-start(bf16[512,512]{1,0:T(8,128)(2,1)} %d0.1) | copy-start | bytes 1572868
  104.4 23.9 %all-to-all-start.2 = ((bf16[4,4,48,1024]{3,2,1,0:T(8,128)(2,1)}), bf16[4,4,48,1024]{3,2,1,0:T(8,128)(2,1)S(1)}, u32[]{:S(2)}, u32[]{:S(2)}) async-start(bf16[4,4,48,1024]{3,2,1,0:T(8,128)(2,1)} %broadcast_in_dim.55), calls=%async_computation.2 | async-start | bytes 3145728 | tf_op jit(solution)/shard_map/all_to_all | solution.py:178
  108.1 75.4 %all-gather.8.cloned.1.call-start = ((), (), s32[]{:S(2)}) async-start(), calls=%async_computation.5 | async-start | bytes 3538944 | tf_op jit(solution)/shard_map/all_gather | solution.py:292
  128.4 30.0 %copy-start = (bf16[4,4,48,1024]{3,2,1,0:T(8,128)(2,1)}, bf16[4,4,48,1024]{3,2,1,0:T(8,128)(2,1)S(1)}, u32[]{:S(2)}) copy-start(bf16[4,4,48,1024]{3,2,1,0:T(8,128)(2,1)S(1)} %all-to-all-done.2.g) | copy-start | bytes 4718596
  128.4 30.0 %collective-permute-start.4 = (bf16[4,4,48,1024]{3,2,1,0:T(8,128)(2,1)S(1)}, bf16[4,4,48,1024]{3,2,1,0:T(8,128)(2,1)}, u32[]{:S(2)}, u32[]{:S(2)}) collective-permute-start(bf16[4,4,48,1024]{3,2,1,0:T(8,128)(2,1)S(1)} %all-to-all-done.2.g), channel_id=1, source_target_pairs={{0,2},{2,0},{1,3},{3,1},{4,6},{6,4},{5,7},{7,5},{8,10},{10,8},{9,1... | collective-permute-start | bytes 4718600 | tf_op jit(solution)/shard_map/ppermute | solution.py:291
  128.5 17.4 %collective-permute-start.5 = (bf16[512,512]{1,0:T(8,128)(2,1)S(1)}, bf16[512,512]{1,0:T(8,128)(2,1)S(1)}, u32[]{:S(2)}, u32[]{:S(2)}) collective-permute-start(bf16[512,512]{1,0:T(8,128)(2,1)S(1)} %copy-done.1), channel_id=1, source_target_pairs={{0,16},{16,32},{32,48},{48,0},{1,17},{17,33},{33,49},{49,1},{2,18}... | collective-permute-start | bytes 1572872 | tf_op jit(solution)/shard_map/ppermute | solution.py:203
  132.7 14.8 %collective-permute-start.6 = (bf16[512,512]{1,0:T(8,128)(2,1)S(1)}, bf16[512,512]{1,0:T(8,128)(2,1)S(1)}, u32[]{:S(2)}, u32[]{:S(2)}) collective-permute-start(bf16[512,512]{1,0:T(8,128)(2,1)S(1)} %copy-done.1), channel_id=1, source_target_pairs={{0,48},{16,0},{32,16},{48,32},{1,49},{17,1},{33,17},{49,33},{2,50}... | collective-permute-start | bytes 1572872 | tf_op jit(solution)/shard_map/ppermute | solution.py:203
  133.4 24.9 %collective-permute-start.7 = (bf16[512,512]{1,0:T(8,128)(2,1)S(1)}, bf16[512,512]{1,0:T(8,128)(2,1)}, u32[]{:S(2)}, u32[]{:S(2)}) collective-permute-start(bf16[512,512]{1,0:T(8,128)(2,1)S(1)} %copy-done.1), channel_id=1, source_target_pairs={{0,32},{16,48},{32,0},{48,16},{1,33},{17,49},{33,1},{49,17},{2,34}... | collective-permute-start | bytes 1572872 | tf_op jit(solution)/shard_map/ppermute | solution.py:203
  145.8 12.5 %copy-start.3 = (bf16[512,512]{1,0:T(8,128)(2,1)}, bf16[512,512]{1,0:T(8,128)(2,1)S(1)}, u32[]{:S(2)}) copy-start(bf16[512,512]{1,0:T(8,128)(2,1)S(1)} %collective-permute-done.5.d1) | copy-start | bytes 1572868
  147.5 10.9 %copy-start.4 = (bf16[512,512]{1,0:T(8,128)(2,1)}, bf16[512,512]{1,0:T(8,128)(2,1)S(1)}, u32[]{:S(2)}) copy-start(bf16[512,512]{1,0:T(8,128)(2,1)S(1)} %collective-permute-done.6.d2) | copy-start | bytes 1572868
  169.3 28.9 %all-to-all-start.3 = ((bf16[4,96,2560]{2,1,0:T(8,128)(2,1)}), bf16[4,96,2560]{2,1,0:T(8,128)(2,1)S(1)}, u32[]{:S(2)}, u32[]{:S(2)}) async-start(bf16[4,96,2560]{2,1,0:T(8,128)(2,1)} %bitcast.62), calls=%async_computation.3 | async-start | bytes 3932160 | tf_op jit(solution)/shard_map/all_to_all | solution.py:308
  183.5 15.1 %copy-start.2 = (f32[96,2560]{1,0:T(8,128)S(1)}, f32[96,2560]{1,0:T(8,128)}, u32[]{:S(2)}) copy-start(f32[96,2560]{1,0:T(8,128)} %get-tuple-element.17) | copy-start | bytes 2949124
Sparse Core Ops, SparseCore 0:
  9.6 96.7 all-gather.5
  128.5 28.9 all-gather.7
where the time goes:
time: 208 us; the launch traced here: 207 us
  waiting for transfers between devices  99.9 us (48%)
  Pallas kernels  33.8 us (16%)
  starting transfers between devices  32 us (15%)
  between operations  14.3 us (7%)
  other arithmetic  13.4 us (6%)
  blocking collectives  9.14 us (4%)
  local copies, waits for them, and re-layouts  4.87 us (2%)
    all_to_all x1, waiting for transfers between devices, step(): pieces = lax.all_to_all(both, 'z', 0, 0, tiled=True)  38.4 us
    ppermute x6, waiting for transfers between devices, shifted(): return lax.ppermute(value, 'x', [(x, (x + k) % 4) for x in range(4)])  33.7 us
    all_to_all x1, waiting for transfers between devices, to_line(): lax.all_to_all(jnp.broadcast_to(value[None], (4, *value.shape)), axis, 0,...  17.5 us
    pallas_call x2, Pallas kernels, half_scores(): pl.pallas_call(body, out_shape=jax.ShapeDtypeStruct((4, 4, part, 2 * pass...  11.8 us
    ppermute x6, starting transfers between devices, shifted(): return lax.ppermute(value, 'x', [(x, (x + k) % 4) for x in range(4)])  11.3 us
    pallas_call x1, Pallas kernels, passage_gradients(): pl.pallas_call(body, grid=(tiles + 1,), out_shape=(jax.ShapeDtypeStruct((...  11.1 us
    pallas_call x1, Pallas kernels, query_gradients(): pl.pallas_call(body, out_shape=(jax.ShapeDtypeStruct((rows, terms + width...  10.9 us
    all_gather x1, blocking collectives, step(): all_loss = lax.all_gather(loss, RED, axis=0)  9.14 us
  transfers between devices with their start and end apart: 14, of which 10 were waited for; matrix products, arithmetic and copies ran while one was open for 8% of the time, Pallas kernels for 16%

commit v1 on v0

--- a/solution.py
+++ b/solution.py
@@ -54,12 +54,16 @@
     tiles = terms // width
     rows, own_rows = 8 * part, 2 * part
 
-    def body(place_ref, g, other, lex, d0, d1, d2, d3, out, own, left, sums):
+    def body(place_ref, core_ref, ex_ref, g, other, lex, d0, d1, d2, d3, out, own, left, sums):
         dense = (d0, d1, d2, d3)
         step = pl.program_id(0)
 
+        def slot_of(x):
+            away = (x + 4 - ex_ref[0]) % 4
+            return jnp.where(away == 2, 3, jnp.where(away == 3, 1, away * 2))
+
         def arrange(low, lines):
-            for source, c in ((g, place_ref[1]), (other, 1 - place_ref[1])):
+            for source, c in ((g, core_ref[0]), (other, 1 - core_ref[0])):
                 at = pl.multiple_of(c * 4 * part, 4 * part)
                 for x in range(4):
                     left[pl.ds(at, 4 * part), x * passages : (x + 1) * passages] = source[
@@ -68,7 +72,7 @@
 
         @pl.when(step == 0)
         def _():
-            arrange(passages, [place_ref[2 + x] for x in range(4)])
+            arrange(passages, [slot_of(x) for x in range(4)])
 
         def finish():
             out[...] = sums[...].astype(out.dtype)
@@ -98,19 +102,19 @@
             jax.ShapeDtypeStruct((own_rows, terms + width), jnp.float32),
         ),
         grid_spec=pltpu.PrefetchScalarGridSpec(
-            num_scalar_prefetch=1,
+            num_scalar_prefetch=3,
             grid=(tiles + 1,),
             in_specs=[
-                pl.BlockSpec(grads.shape, lambda i, h: (0, 0, 0, 0)),
-                pl.BlockSpec(grads.shape, lambda i, h: (0, 0, 0, 0)),
+                pl.BlockSpec(grads.shape, lambda i, *h: (0, 0, 0, 0)),
+                pl.BlockSpec(grads.shape, lambda i, *h: (0, 0, 0, 0)),
                 pl.BlockSpec(
-                    (4, passages, width), lambda i, h: (0, 0, jnp.minimum(i, tiles - 1))
+                    (4, passages, width), lambda i, *h: (0, 0, jnp.minimum(i, tiles - 1))
                 ),
             ]
-            + [pl.BlockSpec((passages, width), lambda i, h: (0, 0))] * 4,
+            + [pl.BlockSpec((passages, width), lambda i, *h: (0, 0))] * 4,
             out_specs=(
-                pl.BlockSpec((rows, width), lambda i, h: (0, i)),
-                pl.BlockSpec((own_rows, width), lambda i, h: (0, i)),
+                pl.BlockSpec((rows, width), lambda i, *h: (0, i)),
+                pl.BlockSpec((own_rows, width), lambda i, *h: (0, i)),
             ),
             scratch_shapes=[
                 pltpu.VMEM((rows, 4 * passages), jnp.bfloat16),
@@ -118,7 +122,7 @@
             ],
         ),
         name="query_gradients",
-    )(place, grads, partner, passage_lex, *passage_dense)
+    )(*place, grads, partner, passage_lex, *passage_dense)
 
 
 def passage_gradients(grads, query_lex, query_dense):
@@ -205,8 +209,6 @@
     both, passage_later = lax.optimization_barrier((both, passage_dense))
     pieces = lax.all_to_all(both, "z", 0, 0, tiled=True)
     near_dense = [shifted(passage_later, 1), shifted(passage_later, 3)]
-    far_dense = shifted(passage_later, 2)
-    line_dense = [passage_dense, *near_dense, far_dense]
     scores4 = pieces.sum(axis=0)
     scores2 = scores4.reshape(rows, 2 * local_passages)
     dense = scores2[:, :local_passages]
@@ -286,7 +288,10 @@
             )
         )
     line_grads = jnp.stack(line_grads)
+    line_grads, passage_far = lax.optimization_barrier((line_grads, passage_dense))
     line_grads = to_line(line_grads, "z")
+    far_dense = shifted(passage_far, 2)
+    line_dense = [passage_dense, *near_dense, far_dense]
     line_grads, grads = lax.optimization_barrier((line_grads, grads))
     partner_grads = lax.ppermute(line_grads, "core", [(0, 1), (1, 0)])
     own_grads = lax.all_gather(grads, RED, axis=0)
@@ -294,12 +299,8 @@
     shape = (4, 2, 4, part, 2 * local_passages)
     place = lax.axis_index(COLUMN)
 
-    def slot_of(x):
-        away = (x + 4 - ex) % 4
-        return jnp.where(away == 2, 3, jnp.where(away == 3, 1, away * 2))
-
     sums, own = query_gradients(
-        jnp.stack([place, core] + [slot_of(x) for x in range(4)]).astype(jnp.int32),
+        [scalar.astype(jnp.int32)[None] for scalar in (place, core, ex)],
         line_grads,
         partner_grads,
         line_lex,

time: 208 us -> 207 us (level)
  no operation moved by 1% of the time
where the time goes in v1:
time: 207 us
  waiting for transfers between devices  100 us (48%)
  Pallas kernels  33.1 us (16%)
  starting transfers between devices  32.1 us (16%)
  between operations  14.3 us (7%)
  other arithmetic  13.9 us (7%)
  blocking collectives  9.15 us (4%)
  local copies, waits for them, and re-layouts  4.2 us (2%)
    all_to_all x1, waiting for transfers between devices, step(): pieces = lax.all_to_all(both, 'z', 0, 0, tiled=True)  38.4 us
    ppermute x6, waiting for transfers between devices, shifted(): return lax.ppermute(value, 'x', [(x, (x + k) % 4) for x in range(4)])  34.3 us
    all_to_all x1, waiting for transfers between devices, to_line(): lax.all_to_all(jnp.broadcast_to(value[None], (4, *value.shape)), axis, 0,...  16.9 us
    pallas_call x2, Pallas kernels, half_scores(): pl.pallas_call(body, out_shape=jax.ShapeDtypeStruct((4, 4, part, 2 * pass...  11.8 us
    ppermute x6, starting transfers between devices, shifted(): return lax.ppermute(value, 'x', [(x, (x + k) % 4) for x in range(4)])  11.3 us
    pallas_call x1, Pallas kernels, passage_gradients(): pl.pallas_call(body, grid=(tiles + 1,), out_shape=(jax.ShapeDtypeStruct((...  11.1 us
    pallas_call x1, Pallas kernels, query_gradients(): pl.pallas_call(body, out_shape=(jax.ShapeDtypeStruct((rows, terms + width...  10.3 us
    all_gather x1, blocking collectives, step(): all_loss = lax.all_gather(loss, RED, axis=0)  9.15 us
  transfers between devices with their start and end apart: 14, of which 10 were waited for; matrix products, arithmetic and copies ran while one was open for 8% of the time, Pallas kernels for 16%

profile of v1, /device:TPU:0, one launch (start us, length us, event | category | flops | bytes accessed | tf_op | source)
XLA Modules:
  0.0 206.8 jit_solution(2989372364176619171)
XLA Ops:
  7.9 5.9 %half_scores.2 = f32[4,4,48,1024]{3,2,1,0:T(8,128)} custom-call(s32[1]{0:T(128)} %bitcast.half_ref, bf16[1536,2048]{1,0:T(8,128)(2,1)} %ql.5, bf16[1536,512]{1,0:T(8,128)(2,1)} %qd.5, bf16[512,2048]{1,0:T(8,128)(2,1)} %pl_.3, bf16[512,512]{1,0:T(8,128)(2,1)} %d0.1), custom_call_target="tpu_custom_call" | custom-call | tf_op jit(solution)/shard_map/half_scores/pallas_call | solution.py:33
  13.8 5.9 %half_scores.3 = f32[4,4,48,1024]{3,2,1,0:T(8,128)} custom-call(s32[1]{0:T(128)} %bitcast.1.half_ref.core_ref, bf16[1536,2048]{1,0:T(8,128)(2,1)} %ql.5, bf16[1536,512]{1,0:T(8,128)(2,1)} %qd.5, bf16[512,2048]{1,0:T(8,128)(2,1)} %pl_.3, bf16[512,512]{1,0:T(8,128)(2,1)} %d0.1), custom_call_target="tpu_custom_call" | custom-call | tf_op jit(solution)/shard_map/half_scores/pallas_call | solution.py:33
  19.7 4.6 %add.243 = f32[4,4,48,1024]{3,2,1,0:T(8,128)} add(f32[4,4,48,1024]{3,2,1,0:T(8,128)S(1)} %collective-permute-done, f32[4,4,48,1024]{3,2,1,0:T(8,128)} %half_scores.3) | non-fusion elementwise | flops 786432 | bytes 9437184 | tf_op jit(solution)/shard_map/add | solution.py:204
  24.3 5.6 %all-to-all-start = ((f32[4,4,48,1024]{3,2,1,0:T(8,128)}), f32[4,4,48,1024]{3,2,1,0:T(8,128)}, u32[]{:S(2)}, u32[]{:S(2)}) async-start(f32[4,4,48,1024]{3,2,1,0:T(8,128)} %add.243), calls=%async_computation | async-start | bytes 6291456 | tf_op jit(solution)/shard_map/all_to_all | solution.py:210
  30.2 38.4 %all-to-all-done = f32[4,4,48,1024]{3,2,1,0:T(8,128)} async-done(((f32[4,4,48,1024]{3,2,1,0:T(8,128)}), f32[4,4,48,1024]{3,2,1,0:T(8,128)}, u32[]{:S(2)}, u32[]{:S(2)}) %all-to-all-start) | async-done | bytes 3145760 | tf_op jit(solution)/shard_map/all_to_all | solution.py:210
  68.6 2.4 %reduce_sum.126 = f32[4,48,1024]{2,1,0:T(8,128)S(1)} reduce(f32[4,4,48,1024]{3,2,1,0:T(8,128)} %all-to-all-done, f32[]{:T(128)} %constant.129.clone.1), dimensions={0}, to_apply=%region_0.0 | reduce | flops 589824 | bytes 3932164 | tf_op jit(solution)/shard_map/reduce_sum | solution.py:212
  72.1 0.7 broadcast_in_dim.60
  72.8 7.0 %all-to-all-start.1 = ((f32[16,11,192]{2,1,0:T(8,128)}), f32[16,11,192]{2,1,0:T(8,128)S(1)}, u32[]{:S(2)}, u32[]{:S(2)}) async-start(f32[16,11,192]{2,1,0:T(8,128)} %broadcast_in_dim.60), calls=%async_computation.1 | async-start | bytes 524288 | tf_op jit(solution)/shard_map/all_to_all | solution.py:241
  79.9 3.2 %collective-permute-start.2 = (f32[48,1024]{1,0:T(8,128)S(1)}, f32[48,1024]{1,0:T(8,128)S(1)}, u32[]{:S(2)}, u32[]{:S(2)}) collective-permute-start(f32[48,1024]{1,0:T(8,128)S(1)} %get-tuple-element.44), channel_id=1, source_target_pairs={{0,48},{16,0},{32,16},{48,32},{1,49},{17,1},{33,17},{49,33},{2,50}... | collective-permute-start | bytes 589832 | tf_op jit(solution)/shard_map/ppermute | solution.py:207
  83.1 0.9 collective-permute-start.3
  84.0 0.9 collective-permute-start.1
  84.8 6.0 %all-to-all-done.1 = f32[16,11,192]{2,1,0:T(8,128)S(1)} async-done(((f32[16,11,192]{2,1,0:T(8,128)}), f32[16,11,192]{2,1,0:T(8,128)S(1)}, u32[]{:S(2)}, u32[]{:S(2)}) %all-to-all-start.1) | async-done | bytes 135200 | tf_op jit(solution)/shard_map/all_to_all | solution.py:241
  91.7 5.9 %collective-permute-done.2 = f32[48,1024]{1,0:T(8,128)S(1)} collective-permute-done((f32[48,1024]{1,0:T(8,128)S(1)}, f32[48,1024]{1,0:T(8,128)S(1)}, u32[]{:S(2)}, u32[]{:S(2)}) %collective-permute-start.2) | collective-permute-done | bytes 196640 | tf_op jit(solution)/shard_map/ppermute | solution.py:207
  97.7 1.4 collective-permute-done.3
  99.0 3.6 %collective-permute-done.1 = f32[48,1024]{1,0:T(8,128)S(1)} collective-permute-done((f32[48,1024]{1,0:T(8,128)S(1)}, f32[48,1024]{1,0:T(8,128)S(1)}, u32[]{:S(2)}, u32[]{:S(2)}) %collective-permute-start.1) | collective-permute-done | bytes 196640 | tf_op jit(solution)/shard_map/ppermute | solution.py:207
  103.1 1.3 broadcast_in_dim.64
  104.4 3.7 %all-to-all-start.2 = ((bf16[4,4,48,1024]{3,2,1,0:T(8,128)(2,1)}), bf16[4,4,48,1024]{3,2,1,0:T(8,128)(2,1)S(1)}, u32[]{:S(2)}, u32[]{:S(2)}) async-start(bf16[4,4,48,1024]{3,2,1,0:T(8,128)(2,1)} %broadcast_in_dim.64), calls=%async_computation.2 | async-start | bytes 3145728 | tf_op jit(solution)/shard_map/all_to_all | solution.py:182
  108.2 0.9 slice.133
  109.6 1.0 fusion.4
  110.6 0.8 pad_maximum_fusion.1
  111.4 16.9 %all-to-all-done.2.g = bf16[4,4,48,1024]{3,2,1,0:T(8,128)(2,1)S(1)} async-done(((bf16[4,4,48,1024]{3,2,1,0:T(8,128)(2,1)}), bf16[4,4,48,1024]{3,2,1,0:T(8,128)(2,1)S(1)}, u32[]{:S(2)}, u32[]{:S(2)}) %all-to-all-start.2) | async-done | bytes 1572896 | tf_op jit(solution)/shard_map/all_to_all | solution.py:182
  128.5 4.2 %collective-permute-start.5 = (bf16[512,512]{1,0:T(8,128)(2,1)S(1)}, bf16[512,512]{1,0:T(8,128)(2,1)S(1)}, u32[]{:S(2)}, u32[]{:S(2)}) collective-permute-start(bf16[512,512]{1,0:T(8,128)(2,1)S(1)} %copy-done.1), channel_id=1, source_target_pairs={{0,16},{16,32},{32,48},{48,0},{1,17},{17,33},{33,49},{49,1},{2,18}... | collective-permute-start | bytes 1572872 | tf_op jit(solution)/shard_map/ppermute | solution.py:207
  133.4 1.5 collective-permute-start.7
  134.9 11.0 %collective-permute-done.5.d1 = bf16[512,512]{1,0:T(8,128)(2,1)S(1)} collective-permute-done((bf16[512,512]{1,0:T(8,128)(2,1)S(1)}, bf16[512,512]{1,0:T(8,128)(2,1)S(1)}, u32[]{:S(2)}, u32[]{:S(2)}) %collective-permute-start.5) | collective-permute-done | bytes 524320 | tf_op jit(solution)/shard_map/ppermute | solution.py:207
  145.8 1.7 collective-permute-done.6.d2
  147.5 10.8 %collective-permute-done.7.d3 = bf16[512,512]{1,0:T(8,128)(2,1)} collective-permute-done((bf16[512,512]{1,0:T(8,128)(2,1)S(1)}, bf16[512,512]{1,0:T(8,128)(2,1)}, u32[]{:S(2)}, u32[]{:S(2)}) %collective-permute-start.7) | collective-permute-done | bytes 524320 | tf_op jit(solution)/shard_map/ppermute | solution.py:207
  158.4 10.3 %query_gradients.1 = (bf16[384,2560]{1,0:T(8,128)(2,1)}, f32[96,2560]{1,0:T(8,128)}) custom-call(s32[1]{0:T(128)} %bitcast.16.place_ref, s32[1]{0:T(128)} %bitcast.1.half_ref.core_ref, s32[1]{0:T(128)} %bitcast.17.ex_ref, bf16[4,4,48,1024]{3,2,1,0:T(8,128)(2,1)} %copy-done, bf16[4,4,48,1024]{3,2,1,0:T(8,128)(2,1)} %collective-permute-done.4.other, ...), custom_call_target="tpu_custom_call" | custom-call | tf_op jit(solution)/shard_map/query_gradients/pallas_call | solution.py:98
  168.6 4.4 %all-to-all-start.3 = ((bf16[4,96,2560]{2,1,0:T(8,128)(2,1)}), bf16[4,96,2560]{2,1,0:T(8,128)(2,1)S(1)}, u32[]{:S(2)}, u32[]{:S(2)}) async-start(bf16[4,96,2560]{2,1,0:T(8,128)(2,1)} %bitcast.59), calls=%async_computation.3 | async-start | bytes 3932160 | tf_op jit(solution)/shard_map/all_to_all | solution.py:309
  173.0 9.2 %all-gather.2 = f32[8,1,192]{2,1,0:T(1,128)S(1)} all-gather(f32[1,1,192]{2,1,0:T(1,128)S(1)} %copy-done.7), channel_id=1, replica_groups=mesh['yh'=2,'x'=4,'z'=4,'core'=2,'yl'=2] {'z','core'}, dimensions={0}, use_global_device_ids=true | all-gather | bytes 6912 | tf_op jit(solution)/shard_map/all_gather | solution.py:298
  183.0 11.1 %passage_gradients.1 = (f32[512,2048]{1,0:T(8,128)}, f32[512,512]{1,0:T(8,128)}) custom-call(bf16[4,2,4,48,1024]{4,3,2,1,0:T(8,128)(2,1)} %bitcast.58, bf16[1536,2048]{1,0:T(8,128)(2,1)} %ql.5, bf16[1536,512]{1,0:T(8,128)(2,1)} %qd.5), custom_call_target="tpu_custom_call" | custom-call | tf_op jit(solution)/shard_map/passage_gradients/pallas_call | solution.py:160
  194.1 3.6 %all-to-all-done.3 = bf16[4,96,2560]{2,1,0:T(8,128)(2,1)S(1)} async-done(((bf16[4,96,2560]{2,1,0:T(8,128)(2,1)}), bf16[4,96,2560]{2,1,0:T(8,128)(2,1)S(1)}, u32[]{:S(2)}, u32[]{:S(2)}) %all-to-all-start.3) | async-done | bytes 1966112 | tf_op jit(solution)/shard_map/all_to_all | solution.py:309
  198.1 1.0 slice_add_fusion
  (63 shorter events, 7.0 us)
Async XLA Ops:
  7.2 151.2 %all-gather.6.cloned.1.call-start = ((), (), s32[]{:S(2)}) async-start(), calls=%async_computation.4 | async-start | bytes 10485760 | tf_op jit(solution)/shard_map/all_gather | solution.py:196
  13.8 5.9 %collective-permute-start = (f32[4,4,48,1024]{3,2,1,0:T(8,128)}, f32[4,4,48,1024]{3,2,1,0:T(8,128)S(1)}, u32[]{:S(2)}, u32[]{:S(2)}) collective-permute-start(f32[4,4,48,1024]{3,2,1,0:T(8,128)} %half_scores.2), channel_id=1, source_target_pairs={{0,2},{2,0},{1,3},{3,1},{4,6},{6,4},{5,7},{7,5},{8,10},{10,8},{9,1... | collective-permute-start | bytes 9437192 | tf_op jit(solution)/shard_map/ppermute | solution.py:203
  24.3 5.6 %copy-start.6 = (s32[1536]{0:T(1024)S(1)}, s32[1536]{0:T(1024)}, u32[]{:S(2)}) copy-start(s32[1536]{0:T(1024)} %param.9) | copy-start | bytes 18436
  24.3 44.3 %all-to-all-start = ((f32[4,4,48,1024]{3,2,1,0:T(8,128)}), f32[4,4,48,1024]{3,2,1,0:T(8,128)}, u32[]{:S(2)}, u32[]{:S(2)}) async-start(f32[4,4,48,1024]{3,2,1,0:T(8,128)} %add.243), calls=%async_computation | async-start | bytes 6291456 | tf_op jit(solution)/shard_map/all_to_all | solution.py:210
  30.1 41.7 %copy-start.5 = (s32[192]{0:T(256)}, s32[192]{0:T(256)S(1)}, u32[]{:S(2)}) copy-start(s32[192]{0:T(256)S(1)} %eq.36) | copy-start | bytes 2308
  72.8 18.0 %all-to-all-start.1 = ((f32[16,11,192]{2,1,0:T(8,128)}), f32[16,11,192]{2,1,0:T(8,128)S(1)}, u32[]{:S(2)}, u32[]{:S(2)}) async-start(f32[16,11,192]{2,1,0:T(8,128)} %broadcast_in_dim.60), calls=%async_computation.1 | async-start | bytes 524288 | tf_op jit(solution)/shard_map/all_to_all | solution.py:241
  79.9 17.6 %collective-permute-start.2 = (f32[48,1024]{1,0:T(8,128)S(1)}, f32[48,1024]{1,0:T(8,128)S(1)}, u32[]{:S(2)}, u32[]{:S(2)}) collective-permute-start(f32[48,1024]{1,0:T(8,128)S(1)} %get-tuple-element.44), channel_id=1, source_target_pairs={{0,48},{16,0},{32,16},{48,32},{1,49},{17,1},{33,17},{49,33},{2,50}... | collective-permute-start | bytes 589832 | tf_op jit(solution)/shard_map/ppermute | solution.py:207
  83.1 15.9 %collective-permute-start.3 = (f32[48,1024]{1,0:T(8,128)S(1)}, f32[48,1024]{1,0:T(8,128)S(1)}, u32[]{:S(2)}, u32[]{:S(2)}) collective-permute-start(f32[48,1024]{1,0:T(8,128)S(1)} %get-tuple-element.43), channel_id=1, source_target_pairs={{0,32},{16,48},{32,0},{48,16},{1,33},{17,49},{33,1},{49,17},{2,34}... | collective-permute-start | bytes 589832 | tf_op jit(solution)/shard_map/ppermute | solution.py:207
  84.0 18.7 %collective-permute-start.1 = (f32[48,1024]{1,0:T(8,128)S(1)}, f32[48,1024]{1,0:T(8,128)S(1)}, u32[]{:S(2)}, u32[]{:S(2)}) collective-permute-start(f32[48,1024]{1,0:T(8,128)S(1)} %get-tuple-element.45), channel_id=1, source_target_pairs={{0,16},{16,32},{32,48},{48,0},{1,17},{17,33},{33,49},{49,1},{2,18}... | collective-permute-start | bytes 589832 | tf_op jit(solution)/shard_map/ppermute | solution.py:207
  104.4 24.1 %copy-start.1 = (bf16[512,512]{1,0:T(8,128)(2,1)S(1)}, bf16[512,512]{1,0:T(8,128)(2,1)}, u32[]{:S(2)}) copy-start(bf16[512,512]{1,0:T(8,128)(2,1)} %d0.1) | copy-start | bytes 1572868
  104.4 23.9 %all-to-all-start.2 = ((bf16[4,4,48,1024]{3,2,1,0:T(8,128)(2,1)}), bf16[4,4,48,1024]{3,2,1,0:T(8,128)(2,1)S(1)}, u32[]{:S(2)}, u32[]{:S(2)}) async-start(bf16[4,4,48,1024]{3,2,1,0:T(8,128)(2,1)} %broadcast_in_dim.64), calls=%async_computation.2 | async-start | bytes 3145728 | tf_op jit(solution)/shard_map/all_to_all | solution.py:182
  108.1 74.9 %all-gather.8.cloned.1.call-start = ((), (), s32[]{:S(2)}) async-start(), calls=%async_computation.5 | async-start | bytes 3538944 | tf_op jit(solution)/shard_map/all_gather | solution.py:297
  128.4 30.0 %copy-start = (bf16[4,4,48,1024]{3,2,1,0:T(8,128)(2,1)}, bf16[4,4,48,1024]{3,2,1,0:T(8,128)(2,1)S(1)}, u32[]{:S(2)}) copy-start(bf16[4,4,48,1024]{3,2,1,0:T(8,128)(2,1)S(1)} %all-to-all-done.2.g) | copy-start | bytes 4718596
  128.4 30.0 %collective-permute-start.4 = (bf16[4,4,48,1024]{3,2,1,0:T(8,128)(2,1)S(1)}, bf16[4,4,48,1024]{3,2,1,0:T(8,128)(2,1)}, u32[]{:S(2)}, u32[]{:S(2)}) collective-permute-start(bf16[4,4,48,1024]{3,2,1,0:T(8,128)(2,1)S(1)} %all-to-all-done.2.g), channel_id=1, source_target_pairs={{0,2},{2,0},{1,3},{3,1},{4,6},{6,4},{5,7},{7,5},{8,10},{10,8},{9,1... | collective-permute-start | bytes 4718600 | tf_op jit(solution)/shard_map/ppermute | solution.py:296
  128.5 17.4 %collective-permute-start.5 = (bf16[512,512]{1,0:T(8,128)(2,1)S(1)}, bf16[512,512]{1,0:T(8,128)(2,1)S(1)}, u32[]{:S(2)}, u32[]{:S(2)}) collective-permute-start(bf16[512,512]{1,0:T(8,128)(2,1)S(1)} %copy-done.1), channel_id=1, source_target_pairs={{0,16},{16,32},{32,48},{48,0},{1,17},{17,33},{33,49},{49,1},{2,18}... | collective-permute-start | bytes 1572872 | tf_op jit(solution)/shard_map/ppermute | solution.py:207
  132.7 14.8 %collective-permute-start.6 = (bf16[512,512]{1,0:T(8,128)(2,1)S(1)}, bf16[512,512]{1,0:T(8,128)(2,1)S(1)}, u32[]{:S(2)}, u32[]{:S(2)}) collective-permute-start(bf16[512,512]{1,0:T(8,128)(2,1)S(1)} %copy-done.1), channel_id=1, source_target_pairs={{0,48},{16,0},{32,16},{48,32},{1,49},{17,1},{33,17},{49,33},{2,50}... | collective-permute-start | bytes 1572872 | tf_op jit(solution)/shard_map/ppermute | solution.py:207
  133.4 24.9 %collective-permute-start.7 = (bf16[512,512]{1,0:T(8,128)(2,1)S(1)}, bf16[512,512]{1,0:T(8,128)(2,1)}, u32[]{:S(2)}, u32[]{:S(2)}) collective-permute-start(bf16[512,512]{1,0:T(8,128)(2,1)S(1)} %copy-done.1), channel_id=1, source_target_pairs={{0,32},{16,48},{32,0},{48,16},{1,33},{17,49},{33,1},{49,17},{2,34}... | collective-permute-start | bytes 1572872 | tf_op jit(solution)/shard_map/ppermute | solution.py:207
  145.8 12.5 %copy-start.3 = (bf16[512,512]{1,0:T(8,128)(2,1)}, bf16[512,512]{1,0:T(8,128)(2,1)S(1)}, u32[]{:S(2)}) copy-start(bf16[512,512]{1,0:T(8,128)(2,1)S(1)} %collective-permute-done.5.d1) | copy-start | bytes 1572868
  147.5 10.9 %copy-start.4 = (bf16[512,512]{1,0:T(8,128)(2,1)}, bf16[512,512]{1,0:T(8,128)(2,1)S(1)}, u32[]{:S(2)}) copy-start(bf16[512,512]{1,0:T(8,128)(2,1)S(1)} %collective-permute-done.6.d2) | copy-start | bytes 1572868
  168.6 4.4 %copy-start.7 = (f32[1,1,192]{2,1,0:T(1,128)S(1)}, f32[1,1,192]{2,1,0:T(1,128)}, u32[]{:S(2)}) copy-start(f32[1,1,192]{2,1,0:T(1,128)} %get-tuple-element.59) | copy-start | bytes 2308
  168.6 29.0 %all-to-all-start.3 = ((bf16[4,96,2560]{2,1,0:T(8,128)(2,1)}), bf16[4,96,2560]{2,1,0:T(8,128)(2,1)S(1)}, u32[]{:S(2)}, u32[]{:S(2)}) async-start(bf16[4,96,2560]{2,1,0:T(8,128)(2,1)} %bitcast.59), calls=%async_computation.3 | async-start | bytes 3932160 | tf_op jit(solution)/shard_map/all_to_all | solution.py:309
  183.0 15.0 %copy-start.2 = (f32[96,2560]{1,0:T(8,128)S(1)}, f32[96,2560]{1,0:T(8,128)}, u32[]{:S(2)}) copy-start(f32[96,2560]{1,0:T(8,128)} %get-tuple-element.21) | copy-start | bytes 2949124
Sparse Core Ops, SparseCore 0:
  9.6 96.7 all-gather.5
  128.5 28.9 all-gather.7

commit v2 on v1

--- a/solution.py
+++ b/solution.py
@@ -54,7 +54,7 @@
     tiles = terms // width
     rows, own_rows = 8 * part, 2 * part
 
-    def body(place_ref, core_ref, ex_ref, g, other, lex, d0, d1, d2, d3, out, own, left, sums):
+    def body(place_ref, core_ref, ex_ref, g, other, lex, d0, d1, d2, d3, out, own, left):
         dense = (d0, d1, d2, d3)
         step = pl.program_id(0)
 
@@ -74,15 +74,17 @@
         def _():
             arrange(passages, [slot_of(x) for x in range(4)])
 
-        def finish():
-            out[...] = sums[...].astype(out.dtype)
-            at = pl.multiple_of(place_ref[0] * own_rows, own_rows)
-            own[...] = sums[pl.ds(at, own_rows), :]
+        def finish(total):
+            out[...] = total.astype(out.dtype)
+            for y in range(4):
+
+                @pl.when(place_ref[0] == y)
+                def _():
+                    own[...] = total[y * own_rows : (y + 1) * own_rows]
 
         @pl.when(step < tiles)
         def _():
-            sums[...] = matmul(left[...], lex[...].reshape(4 * passages, width), NN)
-            finish()
+            finish(matmul(left[...], lex[...].reshape(4 * passages, width), NN))
 
         @pl.when(step == tiles)
         def _():
@@ -92,8 +94,7 @@
                 at = slice(x * passages, (x + 1) * passages)
                 term = matmul(left[:, at], dense[x][...], NN)
                 acc = term if acc is None else acc + term
-            sums[...] = acc
-            finish()
+            finish(acc)
 
     return pl.pallas_call(
         body,
@@ -116,10 +117,7 @@
                 pl.BlockSpec((rows, width), lambda i, *h: (0, i)),
                 pl.BlockSpec((own_rows, width), lambda i, *h: (0, i)),
             ),
-            scratch_shapes=[
-                pltpu.VMEM((rows, 4 * passages), jnp.bfloat16),
-                pltpu.VMEM((rows, width), jnp.float32),
-            ],
+            scratch_shapes=[pltpu.VMEM((rows, 4 * passages), jnp.bfloat16)],
         ),
         name="query_gradients",
     )(*place, grads, partner, passage_lex, *passage_dense)
@@ -310,11 +308,12 @@
     passage_lex_out, passage_dense_out = passage_gradients(
         own_grads.reshape(shape), query_lex, query_dense
     )
-    others = (jnp.arange(4) != place)[:, None, None]
 
     def summed(low, high):
-        wide = jnp.where(others, sums[:, :, low:high].astype(jnp.float32), 0.0)
-        return wide.sum(axis=0) + own[:, low:high]
+        total = own[:, low:high]
+        for k in range(4):
+            total = total + jnp.where(k != place, sums[k, :, low:high].astype(jnp.float32), 0.0)
+        return total
 
     terms = passage_lex.shape[1]
     query_lex_out = summed(0, terms)

time: 207 us -> 207 us (level)
  no operation moved by 1% of the time
where the time goes in v2:
time: 207 us
  waiting for transfers between devices  100 us (48%)
  Pallas kernels  33.2 us (16%)
  starting transfers between devices  32.2 us (16%)
  between operations  14.3 us (7%)
  other arithmetic  13.6 us (7%)
  blocking collectives  8.96 us (4%)
  local copies, waits for them, and re-layouts  4.2 us (2%)
    all_to_all x1, waiting for transfers between devices, step(): pieces = lax.all_to_all(both, 'z', 0, 0, tiled=True)  38.4 us
    ppermute x6, waiting for transfers between devices, shifted(): return lax.ppermute(value, 'x', [(x, (x + k) % 4) for x in range(4)])  34.3 us
    all_to_all x1, waiting for transfers between devices, to_line(): lax.all_to_all(jnp.broadcast_to(value[None], (4, *value.shape)), axis, 0,...  16.9 us
    pallas_call x2, Pallas kernels, half_scores(): pl.pallas_call(body, out_shape=jax.ShapeDtypeStruct((4, 4, part, 2 * pass...  11.8 us
    ppermute x6, starting transfers between devices, shifted(): return lax.ppermute(value, 'x', [(x, (x + k) % 4) for x in range(4)])  11.3 us
    pallas_call x1, Pallas kernels, passage_gradients(): pl.pallas_call(body, grid=(tiles + 1,), out_shape=(jax.ShapeDtypeStruct((...  11.1 us
    pallas_call x1, Pallas kernels, query_gradients(): pl.pallas_call(body, out_shape=(jax.ShapeDtypeStruct((rows, terms + width...  10.3 us
    all_gather x1, blocking collectives, step(): all_loss = lax.all_gather(loss, RED, axis=0)  8.96 us
  transfers between devices with their start and end apart: 14, of which 10 were waited for; matrix products, arithmetic and copies ran while one was open for 8% of the time, Pallas kernels for 16%

profile of v2, /device:TPU:0, one launch (start us, length us, event | category | flops | bytes accessed | tf_op | source)
XLA Modules:
  0.0 206.5 jit_solution(13031858497373271107)
XLA Ops:
  7.9 5.9 %half_scores.2 = f32[4,4,48,1024]{3,2,1,0:T(8,128)} custom-call(s32[1]{0:T(128)} %bitcast.half_ref, bf16[1536,2048]{1,0:T(8,128)(2,1)} %ql.5, bf16[1536,512]{1,0:T(8,128)(2,1)} %qd.5, bf16[512,2048]{1,0:T(8,128)(2,1)} %pl_.3, bf16[512,512]{1,0:T(8,128)(2,1)} %d0.1), custom_call_target="tpu_custom_call" | custom-call | tf_op jit(solution)/shard_map/half_scores/pallas_call | solution.py:33
  13.8 5.9 %half_scores.3 = f32[4,4,48,1024]{3,2,1,0:T(8,128)} custom-call(s32[1]{0:T(128)} %bitcast.1.half_ref.core_ref, bf16[1536,2048]{1,0:T(8,128)(2,1)} %ql.5, bf16[1536,512]{1,0:T(8,128)(2,1)} %qd.5, bf16[512,2048]{1,0:T(8,128)(2,1)} %pl_.3, bf16[512,512]{1,0:T(8,128)(2,1)} %d0.1), custom_call_target="tpu_custom_call" | custom-call | tf_op jit(solution)/shard_map/half_scores/pallas_call | solution.py:33
  19.7 4.6 %add.261 = f32[4,4,48,1024]{3,2,1,0:T(8,128)} add(f32[4,4,48,1024]{3,2,1,0:T(8,128)S(1)} %collective-permute-done, f32[4,4,48,1024]{3,2,1,0:T(8,128)} %half_scores.3) | non-fusion elementwise | flops 786432 | bytes 9437184 | tf_op jit(solution)/shard_map/add | solution.py:202
  24.3 5.6 %all-to-all-start = ((f32[4,4,48,1024]{3,2,1,0:T(8,128)}), f32[4,4,48,1024]{3,2,1,0:T(8,128)}, u32[]{:S(2)}, u32[]{:S(2)}) async-start(f32[4,4,48,1024]{3,2,1,0:T(8,128)} %add.261), calls=%async_computation | async-start | bytes 6291456 | tf_op jit(solution)/shard_map/all_to_all | solution.py:208
  30.2 38.4 %all-to-all-done = f32[4,4,48,1024]{3,2,1,0:T(8,128)} async-done(((f32[4,4,48,1024]{3,2,1,0:T(8,128)}), f32[4,4,48,1024]{3,2,1,0:T(8,128)}, u32[]{:S(2)}, u32[]{:S(2)}) %all-to-all-start) | async-done | bytes 3145760 | tf_op jit(solution)/shard_map/all_to_all | solution.py:208
  68.6 2.4 %reduce_sum.108 = f32[4,48,1024]{2,1,0:T(8,128)S(1)} reduce(f32[4,4,48,1024]{3,2,1,0:T(8,128)} %all-to-all-done, f32[]{:T(128)} %constant.129.clone.1), dimensions={0}, to_apply=%region_0.0 | reduce | flops 589824 | bytes 3932164 | tf_op jit(solution)/shard_map/reduce_sum | solution.py:210
  72.8 7.0 %all-to-all-start.1 = ((f32[16,11,192]{2,1,0:T(8,128)}), f32[16,11,192]{2,1,0:T(8,128)S(1)}, u32[]{:S(2)}, u32[]{:S(2)}) async-start(f32[16,11,192]{2,1,0:T(8,128)} %broadcast_in_dim.49), calls=%async_computation.1 | async-start | bytes 524288 | tf_op jit(solution)/shard_map/all_to_all | solution.py:239
  79.9 3.2 %collective-permute-start.2 = (f32[48,1024]{1,0:T(8,128)S(1)}, f32[48,1024]{1,0:T(8,128)S(1)}, u32[]{:S(2)}, u32[]{:S(2)}) collective-permute-start(f32[48,1024]{1,0:T(8,128)S(1)} %get-tuple-element.44), channel_id=1, source_target_pairs={{0,48},{16,0},{32,16},{48,32},{1,49},{17,1},{33,17},{49,33},{2,50}... | collective-permute-start | bytes 589832 | tf_op jit(solution)/shard_map/ppermute | solution.py:205
  83.1 0.9 collective-permute-start.3
  84.0 0.9 collective-permute-start.1
  84.8 6.0 %all-to-all-done.1 = f32[16,11,192]{2,1,0:T(8,128)S(1)} async-done(((f32[16,11,192]{2,1,0:T(8,128)}), f32[16,11,192]{2,1,0:T(8,128)S(1)}, u32[]{:S(2)}, u32[]{:S(2)}) %all-to-all-start.1) | async-done | bytes 135200 | tf_op jit(solution)/shard_map/all_to_all | solution.py:239
  91.7 5.9 %collective-permute-done.2 = f32[48,1024]{1,0:T(8,128)S(1)} collective-permute-done((f32[48,1024]{1,0:T(8,128)S(1)}, f32[48,1024]{1,0:T(8,128)S(1)}, u32[]{:S(2)}, u32[]{:S(2)}) %collective-permute-start.2) | collective-permute-done | bytes 196640 | tf_op jit(solution)/shard_map/ppermute | solution.py:205
  97.7 1.4 collective-permute-done.3
  99.0 3.6 %collective-permute-done.1 = f32[48,1024]{1,0:T(8,128)S(1)} collective-permute-done((f32[48,1024]{1,0:T(8,128)S(1)}, f32[48,1024]{1,0:T(8,128)S(1)}, u32[]{:S(2)}, u32[]{:S(2)}) %collective-permute-start.1) | collective-permute-done | bytes 196640 | tf_op jit(solution)/shard_map/ppermute | solution.py:205
  103.1 1.3 broadcast_in_dim.52
  104.4 3.7 %all-to-all-start.2 = ((bf16[4,4,48,1024]{3,2,1,0:T(8,128)(2,1)}), bf16[4,4,48,1024]{3,2,1,0:T(8,128)(2,1)S(1)}, u32[]{:S(2)}, u32[]{:S(2)}) async-start(bf16[4,4,48,1024]{3,2,1,0:T(8,128)(2,1)} %broadcast_in_dim.52), calls=%async_computation.2 | async-start | bytes 3145728 | tf_op jit(solution)/shard_map/all_to_all | solution.py:180
  108.2 0.9 slice.157
  109.6 1.0 fusion.4
  110.6 0.8 pad_maximum_fusion.1
  111.4 16.9 %all-to-all-done.2.g = bf16[4,4,48,1024]{3,2,1,0:T(8,128)(2,1)S(1)} async-done(((bf16[4,4,48,1024]{3,2,1,0:T(8,128)(2,1)}), bf16[4,4,48,1024]{3,2,1,0:T(8,128)(2,1)S(1)}, u32[]{:S(2)}, u32[]{:S(2)}) %all-to-all-start.2) | async-done | bytes 1572896 | tf_op jit(solution)/shard_map/all_to_all | solution.py:180
  128.5 4.2 %collective-permute-start.5 = (bf16[512,512]{1,0:T(8,128)(2,1)S(1)}, bf16[512,512]{1,0:T(8,128)(2,1)S(1)}, u32[]{:S(2)}, u32[]{:S(2)}) collective-permute-start(bf16[512,512]{1,0:T(8,128)(2,1)S(1)} %copy-done.1), channel_id=1, source_target_pairs={{0,16},{16,32},{32,48},{48,0},{1,17},{17,33},{33,49},{49,1},{2,18}... | collective-permute-start | bytes 1572872 | tf_op jit(solution)/shard_map/ppermute | solution.py:205
  133.4 1.5 collective-permute-start.7
  134.9 11.0 %collective-permute-done.5.d1 = bf16[512,512]{1,0:T(8,128)(2,1)S(1)} collective-permute-done((bf16[512,512]{1,0:T(8,128)(2,1)S(1)}, bf16[512,512]{1,0:T(8,128)(2,1)S(1)}, u32[]{:S(2)}, u32[]{:S(2)}) %collective-permute-start.5) | collective-permute-done | bytes 524320 | tf_op jit(solution)/shard_map/ppermute | solution.py:205
  145.8 1.7 collective-permute-done.6.d2
  147.5 10.8 %collective-permute-done.7.d3 = bf16[512,512]{1,0:T(8,128)(2,1)} collective-permute-done((bf16[512,512]{1,0:T(8,128)(2,1)S(1)}, bf16[512,512]{1,0:T(8,128)(2,1)}, u32[]{:S(2)}, u32[]{:S(2)}) %collective-permute-start.7) | collective-permute-done | bytes 524320 | tf_op jit(solution)/shard_map/ppermute | solution.py:205
  158.4 10.3 %query_gradients.1 = (bf16[384,2560]{1,0:T(8,128)(2,1)}, f32[96,2560]{1,0:T(8,128)}) custom-call(s32[1]{0:T(128)} %bitcast.16.place_ref, s32[1]{0:T(128)} %bitcast.1.half_ref.core_ref, s32[1]{0:T(128)} %bitcast.17.ex_ref, bf16[4,4,48,1024]{3,2,1,0:T(8,128)(2,1)} %copy-done, bf16[4,4,48,1024]{3,2,1,0:T(8,128)(2,1)} %collective-permute-done.4.other, ...), custom_call_target="tpu_custom_call" | custom-call | tf_op jit(solution)/shard_map/query_gradients/pallas_call | solution.py:99
  168.7 4.4 %all-to-all-start.3 = ((bf16[4,96,2560]{2,1,0:T(8,128)(2,1)}), bf16[4,96,2560]{2,1,0:T(8,128)(2,1)S(1)}, u32[]{:S(2)}, u32[]{:S(2)}) async-start(bf16[4,96,2560]{2,1,0:T(8,128)(2,1)} %bitcast.87), calls=%async_computation.3 | async-start | bytes 3932160 | tf_op jit(solution)/shard_map/all_to_all | solution.py:307
  173.1 9.0 %all-gather.2 = f32[8,1,192]{2,1,0:T(1,128)S(1)} all-gather(f32[1,1,192]{2,1,0:T(1,128)S(1)} %copy-done.7), channel_id=1, replica_groups=mesh['yh'=2,'x'=4,'z'=4,'core'=2,'yl'=2] {'z','core'}, dimensions={0}, use_global_device_ids=true | all-gather | bytes 6912 | tf_op jit(solution)/shard_map/all_gather | solution.py:296
  182.9 11.1 %passage_gradients.1 = (f32[512,2048]{1,0:T(8,128)}, f32[512,512]{1,0:T(8,128)}) custom-call(bf16[4,2,4,48,1024]{4,3,2,1,0:T(8,128)(2,1)} %bitcast.86, bf16[1536,2048]{1,0:T(8,128)(2,1)} %ql.5, bf16[1536,512]{1,0:T(8,128)(2,1)} %qd.5), custom_call_target="tpu_custom_call" | custom-call | tf_op jit(solution)/shard_map/passage_gradients/pallas_call | solution.py:158
  194.0 3.8 %all-to-all-done.3 = bf16[4,96,2560]{2,1,0:T(8,128)(2,1)S(1)} async-done(((bf16[4,96,2560]{2,1,0:T(8,128)(2,1)}), bf16[4,96,2560]{2,1,0:T(8,128)(2,1)S(1)}, u32[]{:S(2)}, u32[]{:S(2)}) %all-to-all-start.3) | async-done | bytes 1966112 | tf_op jit(solution)/shard_map/all_to_all | solution.py:307
  197.7 1.2 bitcast_add_fusion
  198.9 0.8 bitcast_add_fusion.4
  (60 shorter events, 6.5 us)
Async XLA Ops:
  7.2 151.2 %all-gather.6.cloned.1.call-start = ((), (), s32[]{:S(2)}) async-start(), calls=%async_computation.4 | async-start | bytes 10485760 | tf_op jit(solution)/shard_map/all_gather | solution.py:194
  13.8 5.9 %collective-permute-start = (f32[4,4,48,1024]{3,2,1,0:T(8,128)}, f32[4,4,48,1024]{3,2,1,0:T(8,128)S(1)}, u32[]{:S(2)}, u32[]{:S(2)}) collective-permute-start(f32[4,4,48,1024]{3,2,1,0:T(8,128)} %half_scores.2), channel_id=1, source_target_pairs={{0,2},{2,0},{1,3},{3,1},{4,6},{6,4},{5,7},{7,5},{8,10},{10,8},{9,1... | collective-permute-start | bytes 9437192 | tf_op jit(solution)/shard_map/ppermute | solution.py:201
  24.3 5.6 %copy-start.6 = (s32[1536]{0:T(1024)S(1)}, s32[1536]{0:T(1024)}, u32[]{:S(2)}) copy-start(s32[1536]{0:T(1024)} %param.9) | copy-start | bytes 18436
  24.3 44.3 %all-to-all-start = ((f32[4,4,48,1024]{3,2,1,0:T(8,128)}), f32[4,4,48,1024]{3,2,1,0:T(8,128)}, u32[]{:S(2)}, u32[]{:S(2)}) async-start(f32[4,4,48,1024]{3,2,1,0:T(8,128)} %add.261), calls=%async_computation | async-start | bytes 6291456 | tf_op jit(solution)/shard_map/all_to_all | solution.py:208
  30.1 41.7 %copy-start.5 = (s32[192]{0:T(256)}, s32[192]{0:T(256)S(1)}, u32[]{:S(2)}) copy-start(s32[192]{0:T(256)S(1)} %eq.36) | copy-start | bytes 2308
  72.8 18.0 %all-to-all-start.1 = ((f32[16,11,192]{2,1,0:T(8,128)}), f32[16,11,192]{2,1,0:T(8,128)S(1)}, u32[]{:S(2)}, u32[]{:S(2)}) async-start(f32[16,11,192]{2,1,0:T(8,128)} %broadcast_in_dim.49), calls=%async_computation.1 | async-start | bytes 524288 | tf_op jit(solution)/shard_map/all_to_all | solution.py:239
  79.9 17.6 %collective-permute-start.2 = (f32[48,1024]{1,0:T(8,128)S(1)}, f32[48,1024]{1,0:T(8,128)S(1)}, u32[]{:S(2)}, u32[]{:S(2)}) collective-permute-start(f32[48,1024]{1,0:T(8,128)S(1)} %get-tuple-element.44), channel_id=1, source_target_pairs={{0,48},{16,0},{32,16},{48,32},{1,49},{17,1},{33,17},{49,33},{2,50}... | collective-permute-start | bytes 589832 | tf_op jit(solution)/shard_map/ppermute | solution.py:205
  83.1 15.9 %collective-permute-start.3 = (f32[48,1024]{1,0:T(8,128)S(1)}, f32[48,1024]{1,0:T(8,128)S(1)}, u32[]{:S(2)}, u32[]{:S(2)}) collective-permute-start(f32[48,1024]{1,0:T(8,128)S(1)} %get-tuple-element.43), channel_id=1, source_target_pairs={{0,32},{16,48},{32,0},{48,16},{1,33},{17,49},{33,1},{49,17},{2,34}... | collective-permute-start | bytes 589832 | tf_op jit(solution)/shard_map/ppermute | solution.py:205
  84.0 18.7 %collective-permute-start.1 = (f32[48,1024]{1,0:T(8,128)S(1)}, f32[48,1024]{1,0:T(8,128)S(1)}, u32[]{:S(2)}, u32[]{:S(2)}) collective-permute-start(f32[48,1024]{1,0:T(8,128)S(1)} %get-tuple-element.45), channel_id=1, source_target_pairs={{0,16},{16,32},{32,48},{48,0},{1,17},{17,33},{33,49},{49,1},{2,18}... | collective-permute-start | bytes 589832 | tf_op jit(solution)/shard_map/ppermute | solution.py:205
  104.4 24.1 %copy-start.1 = (bf16[512,512]{1,0:T(8,128)(2,1)S(1)}, bf16[512,512]{1,0:T(8,128)(2,1)}, u32[]{:S(2)}) copy-start(bf16[512,512]{1,0:T(8,128)(2,1)} %d0.1) | copy-start | bytes 1572868
  104.4 23.9 %all-to-all-start.2 = ((bf16[4,4,48,1024]{3,2,1,0:T(8,128)(2,1)}), bf16[4,4,48,1024]{3,2,1,0:T(8,128)(2,1)S(1)}, u32[]{:S(2)}, u32[]{:S(2)}) async-start(bf16[4,4,48,1024]{3,2,1,0:T(8,128)(2,1)} %broadcast_in_dim.52), calls=%async_computation.2 | async-start | bytes 3145728 | tf_op jit(solution)/shard_map/all_to_all | solution.py:180
  108.1 74.8 %all-gather.8.cloned.1.call-start = ((), (), s32[]{:S(2)}) async-start(), calls=%async_computation.5 | async-start | bytes 3538944 | tf_op jit(solution)/shard_map/all_gather | solution.py:295
  128.3 30.0 %copy-start = (bf16[4,4,48,1024]{3,2,1,0:T(8,128)(2,1)}, bf16[4,4,48,1024]{3,2,1,0:T(8,128)(2,1)S(1)}, u32[]{:S(2)}) copy-start(bf16[4,4,48,1024]{3,2,1,0:T(8,128)(2,1)S(1)} %all-to-all-done.2.g) | copy-start | bytes 4718596
  128.4 30.0 %collective-permute-start.4 = (bf16[4,4,48,1024]{3,2,1,0:T(8,128)(2,1)S(1)}, bf16[4,4,48,1024]{3,2,1,0:T(8,128)(2,1)}, u32[]{:S(2)}, u32[]{:S(2)}) collective-permute-start(bf16[4,4,48,1024]{3,2,1,0:T(8,128)(2,1)S(1)} %all-to-all-done.2.g), channel_id=1, source_target_pairs={{0,2},{2,0},{1,3},{3,1},{4,6},{6,4},{5,7},{7,5},{8,10},{10,8},{9,1... | collective-permute-start | bytes 4718600 | tf_op jit(solution)/shard_map/ppermute | solution.py:294
  128.5 17.3 %collective-permute-start.5 = (bf16[512,512]{1,0:T(8,128)(2,1)S(1)}, bf16[512,512]{1,0:T(8,128)(2,1)S(1)}, u32[]{:S(2)}, u32[]{:S(2)}) collective-permute-start(bf16[512,512]{1,0:T(8,128)(2,1)S(1)} %copy-done.1), channel_id=1, source_target_pairs={{0,16},{16,32},{32,48},{48,0},{1,17},{17,33},{33,49},{49,1},{2,18}... | collective-permute-start | bytes 1572872 | tf_op jit(solution)/shard_map/ppermute | solution.py:205
  132.7 14.8 %collective-permute-start.6 = (bf16[512,512]{1,0:T(8,128)(2,1)S(1)}, bf16[512,512]{1,0:T(8,128)(2,1)S(1)}, u32[]{:S(2)}, u32[]{:S(2)}) collective-permute-start(bf16[512,512]{1,0:T(8,128)(2,1)S(1)} %copy-done.1), channel_id=1, source_target_pairs={{0,48},{16,0},{32,16},{48,32},{1,49},{17,1},{33,17},{49,33},{2,50}... | collective-permute-start | bytes 1572872 | tf_op jit(solution)/shard_map/ppermute | solution.py:205
  133.4 24.9 %collective-permute-start.7 = (bf16[512,512]{1,0:T(8,128)(2,1)S(1)}, bf16[512,512]{1,0:T(8,128)(2,1)}, u32[]{:S(2)}, u32[]{:S(2)}) collective-permute-start(bf16[512,512]{1,0:T(8,128)(2,1)S(1)} %copy-done.1), channel_id=1, source_target_pairs={{0,32},{16,48},{32,0},{48,16},{1,33},{17,49},{33,1},{49,17},{2,34}... | collective-permute-start | bytes 1572872 | tf_op jit(solution)/shard_map/ppermute | solution.py:205
  145.8 12.5 %copy-start.3 = (bf16[512,512]{1,0:T(8,128)(2,1)}, bf16[512,512]{1,0:T(8,128)(2,1)S(1)}, u32[]{:S(2)}) copy-start(bf16[512,512]{1,0:T(8,128)(2,1)S(1)} %collective-permute-done.5.d1) | copy-start | bytes 1572868
  147.5 10.9 %copy-start.4 = (bf16[512,512]{1,0:T(8,128)(2,1)}, bf16[512,512]{1,0:T(8,128)(2,1)S(1)}, u32[]{:S(2)}) copy-start(bf16[512,512]{1,0:T(8,128)(2,1)S(1)} %collective-permute-done.6.d2) | copy-start | bytes 1572868
  168.7 4.4 %copy-start.7 = (f32[1,1,192]{2,1,0:T(1,128)S(1)}, f32[1,1,192]{2,1,0:T(1,128)}, u32[]{:S(2)}) copy-start(f32[1,1,192]{2,1,0:T(1,128)} %get-tuple-element.59) | copy-start | bytes 2308
  168.7 29.1 %all-to-all-start.3 = ((bf16[4,96,2560]{2,1,0:T(8,128)(2,1)}), bf16[4,96,2560]{2,1,0:T(8,128)(2,1)S(1)}, u32[]{:S(2)}, u32[]{:S(2)}) async-start(bf16[4,96,2560]{2,1,0:T(8,128)(2,1)} %bitcast.87), calls=%async_computation.3 | async-start | bytes 3932160 | tf_op jit(solution)/shard_map/all_to_all | solution.py:307
  182.9 14.9 %copy-start.2 = (f32[96,2560]{1,0:T(8,128)S(1)}, f32[96,2560]{1,0:T(8,128)}, u32[]{:S(2)}) copy-start(f32[96,2560]{1,0:T(8,128)} %get-tuple-element.20) | copy-start | bytes 2949124
Sparse Core Ops, SparseCore 0:
  9.6 96.7 all-gather.5
  128.5 28.9 all-gather.7

commit v3 on v2

--- a/solution.py
+++ b/solution.py
@@ -48,14 +48,14 @@
     )(half, query_lex, query_dense, passage_lex, passage_dense)
 
 
-def query_gradients(place, grads, partner, passage_lex, passage_dense):
+def query_gradients(place, grads, partner, passage_lex, passage_dense, first, tiles):
     part, passages = grads.shape[2], grads.shape[3] // 2
-    terms, width = passage_lex.shape[2], passage_dense[0].shape[1]
-    tiles = terms // width
+    width = passages
+    steps = tiles + (1 if passage_dense else 0)
     rows, own_rows = 8 * part, 2 * part
 
-    def body(place_ref, core_ref, ex_ref, g, other, lex, d0, d1, d2, d3, out, own, left):
-        dense = (d0, d1, d2, d3)
+    def body(place_ref, core_ref, ex_ref, g, other, lex, *rest):
+        *dense, out, own, left = rest
         step = pl.program_id(0)
 
         def slot_of(x):
@@ -86,33 +86,35 @@
         def _():
             finish(matmul(left[...], lex[...].reshape(4 * passages, width), NN))
 
-        @pl.when(step == tiles)
-        def _():
-            arrange(0, range(4))
-            acc = None
-            for x in range(4):
-                at = slice(x * passages, (x + 1) * passages)
-                term = matmul(left[:, at], dense[x][...], NN)
-                acc = term if acc is None else acc + term
-            finish(acc)
+        if dense:
+
+            @pl.when(step == tiles)
+            def _():
+                arrange(0, range(4))
+                acc = None
+                for x in range(4):
+                    at = slice(x * passages, (x + 1) * passages)
+                    term = matmul(left[:, at], dense[x][...], NN)
+                    acc = term if acc is None else acc + term
+                finish(acc)
 
     return pl.pallas_call(
         body,
         out_shape=(
-            jax.ShapeDtypeStruct((rows, terms + width), jnp.bfloat16),
-            jax.ShapeDtypeStruct((own_rows, terms + width), jnp.float32),
+            jax.ShapeDtypeStruct((rows, steps * width), jnp.bfloat16),
+            jax.ShapeDtypeStruct((own_rows, steps * width), jnp.float32),
         ),
         grid_spec=pltpu.PrefetchScalarGridSpec(
             num_scalar_prefetch=3,
-            grid=(tiles + 1,),
+            grid=(steps,),
             in_specs=[
                 pl.BlockSpec(grads.shape, lambda i, *h: (0, 0, 0, 0)),
                 pl.BlockSpec(grads.shape, lambda i, *h: (0, 0, 0, 0)),
                 pl.BlockSpec(
-                    (4, passages, width), lambda i, *h: (0, 0, jnp.minimum(i, tiles - 1))
+                    (4, passages, width), lambda i, *h: (0, 0, first + jnp.minimum(i, tiles - 1))
                 ),
             ]
-            + [pl.BlockSpec((passages, width), lambda i, *h: (0, 0))] * 4,
+            + [pl.BlockSpec((passages, width), lambda i, *h: (0, 0))] * len(passage_dense),
             out_specs=(
                 pl.BlockSpec((rows, width), lambda i, *h: (0, i)),
                 pl.BlockSpec((own_rows, width), lambda i, *h: (0, i)),
@@ -297,27 +299,29 @@
     shape = (4, 2, 4, part, 2 * local_passages)
     place = lax.axis_index(COLUMN)
 
-    sums, own = query_gradients(
-        [scalar.astype(jnp.int32)[None] for scalar in (place, core, ex)],
-        line_grads,
-        partner_grads,
-        line_lex,
-        line_dense,
-    )
-    sums = lax.all_to_all(sums.reshape(4, 2 * part, -1), COLUMN, 0, 0, tiled=True)
+    scalars = [scalar.astype(jnp.int32)[None] for scalar in (place, core, ex)]
+    parts = []
+    for first, tiles, extra in ((0, 2, []), (2, 2, line_dense)):
+        sums, own = query_gradients(
+            scalars, line_grads, partner_grads, line_lex, extra, first, tiles
+        )
+        sums = lax.all_to_all(sums.reshape(4, 2 * part, -1), COLUMN, 0, 0, tiled=True)
+        parts.append((sums, own))
     passage_lex_out, passage_dense_out = passage_gradients(
         own_grads.reshape(shape), query_lex, query_dense
     )
 
-    def summed(low, high):
+    def summed(sums, own, low, high):
         total = own[:, low:high]
         for k in range(4):
             total = total + jnp.where(k != place, sums[k, :, low:high].astype(jnp.float32), 0.0)
         return total
 
-    terms = passage_lex.shape[1]
-    query_lex_out = summed(0, terms)
-    query_dense_out = summed(terms, sums.shape[2])
+    half = parts[0][1].shape[1]
+    query_lex_out = jnp.concatenate(
+        [summed(*parts[0], 0, half), summed(*parts[1], 0, half)], axis=1
+    )
+    query_dense_out = summed(*parts[1], half, half + local_passages)
     ordered = all_loss.reshape(4, 2, 4, part).transpose(1, 2, 0, 3).reshape(queries)
     loss_rows = lax.dynamic_slice_in_dim(ordered, lax.axis_index(RED) * rows, rows)
     return loss_rows, query_lex_out, query_dense_out, passage_lex_out, passage_dense_out

time: 207 us -> 217 us (1.048)
  waiting for transfers between devices: 100 us -> 105 us
  Pallas kernels: 33.2 us -> 35.8 us
  starting transfers between devices: 32.2 us -> 34.5 us
    all_to_all x1 -> x2, starting transfers between devices: 4.41 us -> 8.8 us  [step(): lax.all_to_all(sums.reshape(4, 2 * part, -1), COLUMN, 0, 0, tiled=True)]
    ppermute x6, waiting for transfers between devices: 34.3 us -> 38.3 us  [shifted(): return lax.ppermute(value, 'x', [(x, (x + k) % 4) for x in range(4)])]
    all_to_all x1 -> x2, waiting for transfers between devices: 3.78 us -> 0.01 us  [step(): lax.all_to_all(sums.reshape(4, 2 * part, -1), COLUMN, 0, 0, tiled=True)]
    ppermute x1, waiting for transfers between devices: 0.01 us -> 3.52 us  [step(): partner_grads = lax.ppermute(line_grads, 'core', [(0, 1), (1, 0)])]
    pallas_call x1 -> x2, Pallas kernels: 10.3 us -> 12.9 us  [query_gradients(): pl.pallas_call(body, out_shape=(jax.ShapeDtypeStruct((rows, steps * width...]
  transfers between devices with their start and end apart: 14 -> 15, of which waited for: 10 -> 7; matrix products, arithmetic and copies ran while one was open for 8% -> 6% of each run, Pallas kernels for 16% -> 17%
where the time goes in v3:
time: 217 us; the launch traced here: 215 us
  waiting for transfers between devices  105 us (48%)
  Pallas kernels  35.8 us (16%)
  starting transfers between devices  34.5 us (16%)
  between operations  14.3 us (7%)
  other arithmetic  11.8 us (5%)
  blocking collectives  9.11 us (4%)
  local copies, waits for them, and re-layouts  5.1 us (2%)
    all_to_all x1, waiting for transfers between devices, step(): pieces = lax.all_to_all(both, 'z', 0, 0, tiled=True)  38.4 us
    ppermute x6, waiting for transfers between devices, shifted(): return lax.ppermute(value, 'x', [(x, (x + k) % 4) for x in range(4)])  38.3 us
    all_to_all x1, waiting for transfers between devices, to_line(): lax.all_to_all(jnp.broadcast_to(value[None], (4, *value.shape)), axis, 0,...  18.8 us
    pallas_call x2, Pallas kernels, query_gradients(): pl.pallas_call(body, out_shape=(jax.ShapeDtypeStruct((rows, steps * width...  12.9 us
    pallas_call x2, Pallas kernels, half_scores(): pl.pallas_call(body, out_shape=jax.ShapeDtypeStruct((4, 4, part, 2 * pass...  11.8 us
    pallas_call x1, Pallas kernels, passage_gradients(): pl.pallas_call(body, grid=(tiles + 1,), out_shape=(jax.ShapeDtypeStruct((...  11.1 us
    ppermute x6, starting transfers between devices, shifted(): return lax.ppermute(value, 'x', [(x, (x + k) % 4) for x in range(4)])  9.36 us
    all_gather x1, blocking collectives, step(): all_loss = lax.all_gather(loss, RED, axis=0)  9.11 us
  transfers between devices with their start and end apart: 15, of which 7 were waited for; matrix products, arithmetic and copies ran while one was open for 6% of the time, Pallas kernels for 17%

profile of v3, /device:TPU:0, one launch (start us, length us, event | category | flops | bytes accessed | tf_op | source)
XLA Modules:
  0.0 215.1 jit_solution(9325979955865545822)
XLA Ops:
  7.2 0.7 all-gather.6.cloned.1.call-update
  7.9 5.9 %half_scores.2 = f32[4,4,48,1024]{3,2,1,0:T(8,128)} custom-call(s32[1]{0:T(128)} %bitcast.half_ref, bf16[1536,2048]{1,0:T(8,128)(2,1)} %ql.5, bf16[1536,512]{1,0:T(8,128)(2,1)} %qd.5, bf16[512,2048]{1,0:T(8,128)(2,1)} %pl_.3, bf16[512,512]{1,0:T(8,128)(2,1)} %rest_0_.1), custom_call_target="tpu_custom_call" | custom-call | tf_op jit(solution)/shard_map/half_scores/pallas_call | solution.py:33
  13.8 5.9 %half_scores.3 = f32[4,4,48,1024]{3,2,1,0:T(8,128)} custom-call(s32[1]{0:T(128)} %bitcast.1.half_ref.core_ref, bf16[1536,2048]{1,0:T(8,128)(2,1)} %ql.5, bf16[1536,512]{1,0:T(8,128)(2,1)} %qd.5, bf16[512,2048]{1,0:T(8,128)(2,1)} %pl_.3, bf16[512,512]{1,0:T(8,128)(2,1)} %rest_0_.1), custom_call_target="tpu_custom_call" | custom-call | tf_op jit(solution)/shard_map/half_scores/pallas_call | solution.py:33
  19.7 4.6 %add.273 = f32[4,4,48,1024]{3,2,1,0:T(8,128)} add(f32[4,4,48,1024]{3,2,1,0:T(8,128)S(1)} %collective-permute-done, f32[4,4,48,1024]{3,2,1,0:T(8,128)} %half_scores.3) | non-fusion elementwise | flops 786432 | bytes 9437184 | tf_op jit(solution)/shard_map/add | solution.py:204
  24.3 5.6 %all-to-all-start = ((f32[4,4,48,1024]{3,2,1,0:T(8,128)}), f32[4,4,48,1024]{3,2,1,0:T(8,128)}, u32[]{:S(2)}, u32[]{:S(2)}) async-start(f32[4,4,48,1024]{3,2,1,0:T(8,128)} %add.273), calls=%async_computation | async-start | bytes 6291456 | tf_op jit(solution)/shard_map/all_to_all | solution.py:210
  30.2 38.4 %all-to-all-done = f32[4,4,48,1024]{3,2,1,0:T(8,128)} async-done(((f32[4,4,48,1024]{3,2,1,0:T(8,128)}), f32[4,4,48,1024]{3,2,1,0:T(8,128)}, u32[]{:S(2)}, u32[]{:S(2)}) %all-to-all-start) | async-done | bytes 3145760 | tf_op jit(solution)/shard_map/all_to_all | solution.py:210
  68.6 2.3 %reduce_sum.108 = f32[4,48,1024]{2,1,0:T(8,128)S(1)} reduce(f32[4,4,48,1024]{3,2,1,0:T(8,128)} %all-to-all-done, f32[]{:T(128)} %constant.129.clone.1), dimensions={0}, to_apply=%region_0.0 | reduce | flops 589824 | bytes 3932164 | tf_op jit(solution)/shard_map/reduce_sum | solution.py:212
  72.0 0.7 broadcast_in_dim.53
  72.7 7.0 %all-to-all-start.1 = ((f32[16,11,192]{2,1,0:T(8,128)}), f32[16,11,192]{2,1,0:T(8,128)S(1)}, u32[]{:S(2)}, u32[]{:S(2)}) async-start(f32[16,11,192]{2,1,0:T(8,128)} %broadcast_in_dim.53), calls=%async_computation.1 | async-start | bytes 524288 | tf_op jit(solution)/shard_map/all_to_all | solution.py:241
  79.8 2.0 collective-permute-start.1
  81.8 2.7 %collective-permute-start.3 = (f32[48,1024]{1,0:T(8,128)S(1)}, f32[48,1024]{1,0:T(8,128)S(1)}, u32[]{:S(2)}, u32[]{:S(2)}) collective-permute-start(f32[48,1024]{1,0:T(8,128)S(1)} %get-tuple-element.47), channel_id=1, source_target_pairs={{0,32},{16,48},{32,0},{48,16},{1,33},{17,49},{33,1},{49,17},{2,34}... | collective-permute-start | bytes 589832 | tf_op jit(solution)/shard_map/ppermute | solution.py:207
  84.5 1.5 collective-permute-start.2
  86.0 4.8 %all-to-all-done.1 = f32[16,11,192]{2,1,0:T(8,128)S(1)} async-done(((f32[16,11,192]{2,1,0:T(8,128)}), f32[16,11,192]{2,1,0:T(8,128)S(1)}, u32[]{:S(2)}, u32[]{:S(2)}) %all-to-all-start.1) | async-done | bytes 135200 | tf_op jit(solution)/shard_map/all_to_all | solution.py:241
  91.0 5.6 %collective-permute-done.1 = f32[48,1024]{1,0:T(8,128)S(1)} collective-permute-done((f32[48,1024]{1,0:T(8,128)S(1)}, f32[48,1024]{1,0:T(8,128)S(1)}, u32[]{:S(2)}, u32[]{:S(2)}) %collective-permute-start.1) | collective-permute-done | bytes 196640 | tf_op jit(solution)/shard_map/ppermute | solution.py:207
  96.5 9.8 %collective-permute-done.3 = f32[48,1024]{1,0:T(8,128)S(1)} collective-permute-done((f32[48,1024]{1,0:T(8,128)S(1)}, f32[48,1024]{1,0:T(8,128)S(1)}, u32[]{:S(2)}, u32[]{:S(2)}) %collective-permute-start.3) | collective-permute-done | bytes 196640 | tf_op jit(solution)/shard_map/ppermute | solution.py:207
  106.9 1.3 broadcast_in_dim.56
  108.3 3.6 %all-to-all-start.2 = ((bf16[4,4,48,1024]{3,2,1,0:T(8,128)(2,1)}), bf16[4,4,48,1024]{3,2,1,0:T(8,128)(2,1)S(1)}, u32[]{:S(2)}, u32[]{:S(2)}) async-start(bf16[4,4,48,1024]{3,2,1,0:T(8,128)(2,1)} %broadcast_in_dim.56), calls=%async_computation.2 | async-start | bytes 3145728 | tf_op jit(solution)/shard_map/all_to_all | solution.py:182
  112.3 0.8 pad_maximum_fusion.2
  113.1 18.8 %all-to-all-done.2.g = bf16[4,4,48,1024]{3,2,1,0:T(8,128)(2,1)S(1)} async-done(((bf16[4,4,48,1024]{3,2,1,0:T(8,128)(2,1)}), bf16[4,4,48,1024]{3,2,1,0:T(8,128)(2,1)S(1)}, u32[]{:S(2)}, u32[]{:S(2)}) %all-to-all-start.2) | async-done | bytes 1572896 | tf_op jit(solution)/shard_map/all_to_all | solution.py:182
  132.0 3.5 %collective-permute-done.4.other = bf16[4,4,48,1024]{3,2,1,0:T(8,128)(2,1)} collective-permute-done((bf16[4,4,48,1024]{3,2,1,0:T(8,128)(2,1)S(1)}, bf16[4,4,48,1024]{3,2,1,0:T(8,128)(2,1)}, u32[]{:S(2)}, u32[]{:S(2)}) %collective-permute-start.4) | collective-permute-done | bytes 1572896 | tf_op jit(solution)/shard_map/ppermute | solution.py:296
  135.5 5.7 %query_gradients.2 = (bf16[384,1024]{1,0:T(8,128)(2,1)}, f32[96,1024]{1,0:T(8,128)}) custom-call(s32[1]{0:T(128)} %bitcast.16.place_ref, s32[1]{0:T(128)} %bitcast.1.half_ref.core_ref, s32[1]{0:T(128)} %bitcast.17.ex_ref, bf16[4,4,48,1024]{3,2,1,0:T(8,128)(2,1)} %copy-done, bf16[4,4,48,1024]{3,2,1,0:T(8,128)(2,1)} %collective-permute-done.4.other, ...), custom_call_target="tpu_custom_call" | custom-call | tf_op jit(solution)/shard_map/query_gradients/pallas_call | solution.py:101
  141.2 4.2 %all-to-all-start.3 = ((bf16[4,96,1024]{2,1,0:T(8,128)(2,1)}), bf16[4,96,1024]{2,1,0:T(8,128)(2,1)S(1)}, u32[]{:S(2)}, u32[]{:S(2)}) async-start(bf16[4,96,1024]{2,1,0:T(8,128)(2,1)} %bitcast.105), calls=%async_computation.3 | async-start | bytes 1572864 | tf_op jit(solution)/shard_map/all_to_all | solution.py:308
  145.5 3.2 %collective-permute-start.6 = (bf16[512,512]{1,0:T(8,128)(2,1)S(1)}, bf16[512,512]{1,0:T(8,128)(2,1)S(1)}, u32[]{:S(2)}, u32[]{:S(2)}) collective-permute-start(bf16[512,512]{1,0:T(8,128)(2,1)S(1)} %copy-done.1), channel_id=1, source_target_pairs={{0,48},{16,0},{32,16},{48,32},{1,49},{17,1},{33,17},{49,33},{2,50}... | collective-permute-start | bytes 1572872 | tf_op jit(solution)/shard_map/ppermute | solution.py:207
  148.7 22.9 %collective-permute-done.5.rest_1_ = bf16[512,512]{1,0:T(8,128)(2,1)S(1)} collective-permute-done((bf16[512,512]{1,0:T(8,128)(2,1)S(1)}, bf16[512,512]{1,0:T(8,128)(2,1)S(1)}, u32[]{:S(2)}, u32[]{:S(2)}) %collective-permute-start.5) | collective-permute-done | bytes 524320 | tf_op jit(solution)/shard_map/ppermute | solution.py:207
  171.6 0.8 copy-done.3
  172.5 0.8 copy-done.5
  173.3 7.3 %query_gradients.3 = (bf16[384,1536]{1,0:T(8,128)(2,1)}, f32[96,1536]{1,0:T(8,128)}) custom-call(s32[1]{0:T(128)} %bitcast.16.place_ref, s32[1]{0:T(128)} %bitcast.1.half_ref.core_ref, s32[1]{0:T(128)} %bitcast.17.ex_ref, bf16[4,4,48,1024]{3,2,1,0:T(8,128)(2,1)} %copy-done, bf16[4,4,48,1024]{3,2,1,0:T(8,128)(2,1)} %collective-permute-done.4.other, ...), custom_call_target="tpu_custom_call" | custom-call | tf_op jit(solution)/shard_map/query_gradients/pallas_call | solution.py:101
  180.6 4.6 %all-to-all-start.4 = ((bf16[4,96,1536]{2,1,0:T(8,128)(2,1)}), bf16[4,96,1536]{2,1,0:T(8,128)(2,1)S(1)}, u32[]{:S(2)}, u32[]{:S(2)}) async-start(bf16[4,96,1536]{2,1,0:T(8,128)(2,1)} %bitcast.104), calls=%async_computation.4 | async-start | bytes 2359296 | tf_op jit(solution)/shard_map/all_to_all | solution.py:308
  185.2 9.1 %all-gather.2 = f32[8,1,192]{2,1,0:T(1,128)S(1)} all-gather(f32[1,1,192]{2,1,0:T(1,128)S(1)} %get-tuple-element.63), channel_id=1, replica_groups=mesh['yh'=2,'x'=4,'z'=4,'core'=2,'yl'=2] {'z','core'}, dimensions={0}, use_global_device_ids=true | all-gather | bytes 6912 | tf_op jit(solution)/shard_map/all_gather | solution.py:298
  195.1 11.1 %passage_gradients.1 = (f32[512,2048]{1,0:T(8,128)}, f32[512,512]{1,0:T(8,128)}) custom-call(bf16[4,2,4,48,1024]{4,3,2,1,0:T(8,128)(2,1)} %bitcast.102, bf16[1536,2048]{1,0:T(8,128)(2,1)} %ql.5, bf16[1536,512]{1,0:T(8,128)(2,1)} %qd.5), custom_call_target="tpu_custom_call" | custom-call | tf_op jit(solution)/shard_map/passage_gradients/pallas_call | solution.py:160
  206.6 0.9 pad_maximum_fusion
  207.5 0.8 bitcast_add_fusion.8
  (65 shorter events, 4.0 us)
Async XLA Ops:
  7.2 128.4 %all-gather.6.cloned.1.call-start = ((), (), s32[]{:S(2)}) async-start(), calls=%async_computation.5 | async-start | bytes 10485760 | tf_op jit(solution)/shard_map/all_gather | solution.py:196
  13.8 5.9 %collective-permute-start = (f32[4,4,48,1024]{3,2,1,0:T(8,128)}, f32[4,4,48,1024]{3,2,1,0:T(8,128)S(1)}, u32[]{:S(2)}, u32[]{:S(2)}) collective-permute-start(f32[4,4,48,1024]{3,2,1,0:T(8,128)} %half_scores.2), channel_id=1, source_target_pairs={{0,2},{2,0},{1,3},{3,1},{4,6},{6,4},{5,7},{7,5},{8,10},{10,8},{9,1... | collective-permute-start | bytes 9437192 | tf_op jit(solution)/shard_map/ppermute | solution.py:203
  24.3 5.6 %copy-start.7 = (s32[1536]{0:T(1024)S(1)}, s32[1536]{0:T(1024)}, u32[]{:S(2)}) copy-start(s32[1536]{0:T(1024)} %param.9) | copy-start | bytes 18436
  24.3 44.3 %all-to-all-start = ((f32[4,4,48,1024]{3,2,1,0:T(8,128)}), f32[4,4,48,1024]{3,2,1,0:T(8,128)}, u32[]{:S(2)}, u32[]{:S(2)}) async-start(f32[4,4,48,1024]{3,2,1,0:T(8,128)} %add.273), calls=%async_computation | async-start | bytes 6291456 | tf_op jit(solution)/shard_map/all_to_all | solution.py:210
  72.7 18.0 %all-to-all-start.1 = ((f32[16,11,192]{2,1,0:T(8,128)}), f32[16,11,192]{2,1,0:T(8,128)S(1)}, u32[]{:S(2)}, u32[]{:S(2)}) async-start(f32[16,11,192]{2,1,0:T(8,128)} %broadcast_in_dim.53), calls=%async_computation.1 | async-start | bytes 524288 | tf_op jit(solution)/shard_map/all_to_all | solution.py:241
  79.8 16.7 %collective-permute-start.1 = (f32[48,1024]{1,0:T(8,128)S(1)}, f32[48,1024]{1,0:T(8,128)S(1)}, u32[]{:S(2)}, u32[]{:S(2)}) collective-permute-start(f32[48,1024]{1,0:T(8,128)S(1)} %get-tuple-element.49), channel_id=1, source_target_pairs={{0,16},{16,32},{32,48},{48,0},{1,17},{17,33},{33,49},{49,1},{2,18}... | collective-permute-start | bytes 589832 | tf_op jit(solution)/shard_map/ppermute | solution.py:207
  81.8 24.5 %collective-permute-start.3 = (f32[48,1024]{1,0:T(8,128)S(1)}, f32[48,1024]{1,0:T(8,128)S(1)}, u32[]{:S(2)}, u32[]{:S(2)}) collective-permute-start(f32[48,1024]{1,0:T(8,128)S(1)} %get-tuple-element.47), channel_id=1, source_target_pairs={{0,32},{16,48},{32,0},{48,16},{1,33},{17,49},{33,1},{49,17},{2,34}... | collective-permute-start | bytes 589832 | tf_op jit(solution)/shard_map/ppermute | solution.py:207
  84.5 22.2 %collective-permute-start.2 = (f32[48,1024]{1,0:T(8,128)S(1)}, f32[48,1024]{1,0:T(8,128)S(1)}, u32[]{:S(2)}, u32[]{:S(2)}) collective-permute-start(f32[48,1024]{1,0:T(8,128)S(1)} %get-tuple-element.48), channel_id=1, source_target_pairs={{0,48},{16,0},{32,16},{48,32},{1,49},{17,1},{33,17},{49,33},{2,50}... | collective-permute-start | bytes 589832 | tf_op jit(solution)/shard_map/ppermute | solution.py:207
  108.3 23.6 %all-to-all-start.2 = ((bf16[4,4,48,1024]{3,2,1,0:T(8,128)(2,1)}), bf16[4,4,48,1024]{3,2,1,0:T(8,128)(2,1)S(1)}, u32[]{:S(2)}, u32[]{:S(2)}) async-start(bf16[4,4,48,1024]{3,2,1,0:T(8,128)(2,1)} %broadcast_in_dim.56), calls=%async_computation.2 | async-start | bytes 3145728 | tf_op jit(solution)/shard_map/all_to_all | solution.py:182
  111.8 83.3 %all-gather.8.cloned.1.call-start = ((), (), s32[]{:S(2)}) async-start(), calls=%async_computation.6 | async-start | bytes 3538944 | tf_op jit(solution)/shard_map/all_gather | solution.py:297
  131.9 3.7 %copy-start = (bf16[4,4,48,1024]{3,2,1,0:T(8,128)(2,1)}, bf16[4,4,48,1024]{3,2,1,0:T(8,128)(2,1)S(1)}, u32[]{:S(2)}) copy-start(bf16[4,4,48,1024]{3,2,1,0:T(8,128)(2,1)S(1)} %all-to-all-done.2.g) | copy-start | bytes 4718596
  131.9 3.6 %collective-permute-start.4 = (bf16[4,4,48,1024]{3,2,1,0:T(8,128)(2,1)S(1)}, bf16[4,4,48,1024]{3,2,1,0:T(8,128)(2,1)}, u32[]{:S(2)}, u32[]{:S(2)}) collective-permute-start(bf16[4,4,48,1024]{3,2,1,0:T(8,128)(2,1)S(1)} %all-to-all-done.2.g), channel_id=1, source_target_pairs={{0,2},{2,0},{1,3},{3,1},{4,6},{6,4},{5,7},{7,5},{8,10},{10,8},{9,1... | collective-permute-start | bytes 4718600 | tf_op jit(solution)/shard_map/ppermute | solution.py:296
  135.5 9.9 %copy-start.1 = (bf16[512,512]{1,0:T(8,128)(2,1)S(1)}, bf16[512,512]{1,0:T(8,128)(2,1)}, u32[]{:S(2)}) copy-start(bf16[512,512]{1,0:T(8,128)(2,1)} %rest_0_.1) | copy-start | bytes 1572868
  141.2 39.4 %all-to-all-start.3 = ((bf16[4,96,1024]{2,1,0:T(8,128)(2,1)}), bf16[4,96,1024]{2,1,0:T(8,128)(2,1)S(1)}, u32[]{:S(2)}, u32[]{:S(2)}) async-start(bf16[4,96,1024]{2,1,0:T(8,128)(2,1)} %bitcast.105), calls=%async_computation.3 | async-start | bytes 1572864 | tf_op jit(solution)/shard_map/all_to_all | solution.py:308
  145.4 26.1 %collective-permute-start.5 = (bf16[512,512]{1,0:T(8,128)(2,1)S(1)}, bf16[512,512]{1,0:T(8,128)(2,1)S(1)}, u32[]{:S(2)}, u32[]{:S(2)}) collective-permute-start(bf16[512,512]{1,0:T(8,128)(2,1)S(1)} %copy-done.1), channel_id=1, source_target_pairs={{0,16},{16,32},{32,48},{48,0},{1,17},{17,33},{33,49},{49,1},{2,18}... | collective-permute-start | bytes 1572872 | tf_op jit(solution)/shard_map/ppermute | solution.py:207
  145.5 26.1 %collective-permute-start.6 = (bf16[512,512]{1,0:T(8,128)(2,1)S(1)}, bf16[512,512]{1,0:T(8,128)(2,1)S(1)}, u32[]{:S(2)}, u32[]{:S(2)}) collective-permute-start(bf16[512,512]{1,0:T(8,128)(2,1)S(1)} %copy-done.1), channel_id=1, source_target_pairs={{0,48},{16,0},{32,16},{48,32},{1,49},{17,1},{33,17},{49,33},{2,50}... | collective-permute-start | bytes 1572872 | tf_op jit(solution)/shard_map/ppermute | solution.py:207
  148.7 22.9 %collective-permute-start.7 = (bf16[512,512]{1,0:T(8,128)(2,1)S(1)}, bf16[512,512]{1,0:T(8,128)(2,1)S(1)}, u32[]{:S(2)}, u32[]{:S(2)}) collective-permute-start(bf16[512,512]{1,0:T(8,128)(2,1)S(1)} %copy-done.1), channel_id=1, source_target_pairs={{0,32},{16,48},{32,0},{48,16},{1,33},{17,49},{33,1},{49,17},{2,34}... | collective-permute-start | bytes 1572872 | tf_op jit(solution)/shard_map/ppermute | solution.py:207
  171.6 0.8 copy-start.3
  171.6 1.0 copy-start.4
  172.5 0.8 copy-start.5
  180.6 25.7 %all-to-all-start.4 = ((bf16[4,96,1536]{2,1,0:T(8,128)(2,1)}), bf16[4,96,1536]{2,1,0:T(8,128)(2,1)S(1)}, u32[]{:S(2)}, u32[]{:S(2)}) async-start(bf16[4,96,1536]{2,1,0:T(8,128)(2,1)} %bitcast.104), calls=%async_computation.4 | async-start | bytes 2359296 | tf_op jit(solution)/shard_map/all_to_all | solution.py:308
  195.1 11.1 %copy-start.6 = (f32[96,1024]{1,0:T(8,128)S(1)}, f32[96,1024]{1,0:T(8,128)}, u32[]{:S(2)}) copy-start(f32[96,1024]{1,0:T(8,128)} %get-tuple-element.20) | copy-start | bytes 1179652
  195.1 11.3 %copy-start.2 = (f32[96,1536]{1,0:T(8,128)S(1)}, f32[96,1536]{1,0:T(8,128)}, u32[]{:S(2)}) copy-start(f32[96,1536]{1,0:T(8,128)} %get-tuple-element.24) | copy-start | bytes 1769476
Sparse Core Ops, SparseCore 0:
  9.6 96.7 all-gather.5
  132.0 25.1 all-gather.7
